TPU v7x, 32 devices: a whole 2x2x4 slice. The times are simulated.
32 devices in a mesh: dp: 2 (over y), ctx: 2 (over core), expert: 8 (over z, x).
Axes of the slice: x: 2, y: 2, z: 4, core: 2. Of those that a mesh axis runs over, the one named last changes fastest.
Arguments:
- hidden_in: bfloat16 [4, 1024, 2048], P('dp', ('ctx', 'expert')), may hold values from -9 to 9
- out_grad: bfloat16 [4, 1024, 2048], P('dp', ('ctx', 'expert')), may hold values from -6 to 6
- routes: int32 [4, 1024, 6], P('dp', ('ctx', 'expert')), may hold values from 0 to 15, all different within a row; in each aligned block of 64 rows (0 to 63, 64 to 127, ..., all dimensions but the last counted through in order) at most 32 rows name the same one
- block_order: int32 [4, 4], P('dp'), may hold values from 0 to 3, as said below
- norm_attn: float32 [2048], replicated, may hold values from 0.25 to 1.75
- w_query: bfloat16 [2048, 3072], P(None, 'expert'), may hold values from -0.088388348 to 0.088388348
- w_kv_down: bfloat16 [2048, 576], P('expert'), may hold values from -0.088388348 to 0.088388348
- norm_latent: float32 [512], replicated, may hold values from 0.25 to 1.75
- w_key_up: bfloat16 [512, 2048], P(None, 'expert'), may hold values from -0.25 to 0.25
- w_value_up: bfloat16 [512, 2048], P(None, 'expert'), may hold values from -0.25 to 0.25
- w_out: bfloat16 [2048, 2048], P('expert'), may hold values from -3 to 3
- norm_ffn: float32 [2048], replicated, may hold values from 0.25 to 1.75
- w_router: bfloat16 [2048, 16], replicated, may hold values from -0.25 to 0.25
- shared_gate: bfloat16 [2048, 2816], P(None, 'expert'), may hold values from -0.125 to 0.125
- shared_up: bfloat16 [2048, 2816], P(None, 'expert'), may hold values from -0.125 to 0.125
- shared_down: bfloat16 [2816, 2048], P('expert'), may hold values from -0.109375 to 0.109375
- expert_gate: bfloat16 [16, 2048, 1408], P(('dp', 'expert')), may hold values from -0.125 to 0.125
- expert_up: bfloat16 [16, 2048, 1408], P(('dp', 'expert')), may hold values from -0.125 to 0.125
- expert_down: bfloat16 [16, 1408, 2048], P(('dp', 'expert')), may hold values from -0.15625 to 0.15625
Outputs:
- out_hidden: bfloat16 [4, 1024, 2048], P('dp', ('ctx', 'expert'))
- in_grad: bfloat16 [4, 1024, 2048], P('dp', ('ctx', 'expert'))
- grad_norm_attn: float32 [2048], P('expert')
- grad_query: float32 [2048, 3072], P(None, 'expert')
- grad_kv_down: float32 [2048, 576], P('expert')
- grad_norm_latent: float32 [512], P('expert')
- grad_key_up: float32 [512, 2048], P(None, 'expert')
- grad_value_up: float32 [512, 2048], P(None, 'expert')
- grad_out_proj: float32 [2048, 2048], P('expert')
- grad_norm_ffn: float32 [2048], P('expert')
- grad_router: float32 [2048, 16], P('expert')
- grad_shared_gate: float32 [2048, 2816], P(None, 'expert')
- grad_shared_up: float32 [2048, 2816], P(None, 'expert')
- grad_shared_down: float32 [2816, 2048], P('expert')
- grad_expert_gate: float32 [16, 2048, 1408], P(('dp', 'expert'), 'ctx')
- grad_expert_up: float32 [16, 2048, 1408], P(('dp', 'expert'), 'ctx')
- grad_expert_down: float32 [16, 1408, 2048], P(('dp', 'expert'), 'ctx')
Inputs may be any that keep to these rules, and one draw needn't show every extreme that they name: `routes`: each row names 6 different experts. In the rows of one sequence on one device (64 aligned rows) no expert is named by more than 32 rows, a bound that some block reaches. `block_order`: each sequence's row is a permutation of 0 to 3 in which entries 2 c and 2 c + 1 sum to 3.
All inputs are finite; a program needn't handle non-finite values.
Results may differ from a plain program's by a relative error of at most 0.035.
Values may be sent and summed in bfloat16 or wider, within the bound.
No kernel may reach another device: no remote copies, remote signals or barrier semaphores. Data moves between devices by JAX's collectives and lax.ppermute only.
A program may use at most 320 MiB of HBM per device.

v0:
```python
import functools

import jax
import jax.numpy as jnp
from jax import lax
from jax.experimental import pallas as pl
from jax.experimental.pallas import tpu as pltpu
from jax.sharding import PartitionSpec as P


NOPE = 128
ROPE = 64
VDIM = 128
LATENT = 512
TOP = 6
EPSILON = 1e-06
MASKED = -1e30
BF16 = jnp.bfloat16
F32 = jnp.float32
EXPERT, CTX, DP = "expert", "ctx", "dp"


def product(inputs, matrix):
    return jnp.dot(inputs, matrix, preferred_element_type=F32)


def back_product(gradient, matrix):
    return lax.dot_general(
        gradient,
        matrix,
        (((gradient.ndim - 1,), (1,)), ((), ())),
        preferred_element_type=F32,
    )


def weight_grad(inputs, gradient):
    flat_in = inputs.reshape(-1, inputs.shape[-1])
    flat_grad = gradient.reshape(-1, gradient.shape[-1])
    return lax.dot_general(
        flat_in, flat_grad, (((0,), (0,)), ((), ())), preferred_element_type=F32
    )


def rope_tables(positions):
    inverse = 10000.0 ** (-2.0 * jnp.arange(ROPE // 2, dtype=F32) / ROPE)
    angles = positions.astype(F32)[..., None] * inverse
    return jnp.cos(angles), jnp.sin(angles)


def halves(vectors):
    return vectors[..., : ROPE // 2], vectors[..., ROPE // 2 :]


def rotate(vectors, tables):
    first, second = halves(vectors)
    cosine, sine = tables
    return jnp.concatenate(
        [first * cosine - second * sine, second * cosine + first * sine], axis=-1
    )


def unrotate(gradient, tables):
    first, second = halves(gradient)
    cosine, sine = tables
    return jnp.concatenate(
        [first * cosine + second * sine, second * cosine - first * sine], axis=-1
    )


def norm_back(gradient, inputs, inverse_rms, gain_vec):
    scaled = gradient * gain_vec
    return inverse_rms * scaled - inputs * inverse_rms**3 * jnp.mean(
        inputs * scaled, axis=-1, keepdims=True
    )


def silu_grads(grad_hidden, gate, upward):
    sigmoid_gate = jax.nn.sigmoid(gate)
    grad_gate = grad_hidden * upward * sigmoid_gate * (1.0 + gate * (1.0 - sigmoid_gate))
    grad_upward = grad_hidden * gate * sigmoid_gate
    return (grad_gate.astype(BF16), grad_upward.astype(BF16))


def dot_nt(left, right):
    return lax.dot_general(left, right, (((1,), (1,)), ((), ())), preferred_element_type=F32)


def dot_tn(left, right):
    return lax.dot_general(left, right, (((0,), (0,)), ((), ())), preferred_element_type=F32)


def dot_nn(left, right):
    return lax.dot_general(left, right, (((1,), (0,)), ((), ())), preferred_element_type=F32)


def head_cols(head):
    return slice(head * NOPE, (head + 1) * NOPE)


def rope_cols(heads, head):
    start = heads * NOPE + head * ROPE
    return slice(start, start + ROPE)


def forward_kernel(heads, scale, q_ref, k_ref, v_ref, kr_ref, pq_ref, pk_ref, o_ref, lse_ref):
    allowed = pk_ref[0] <= pq_ref[0]
    for head in range(heads):
        cols = head_cols(head)
        scores = dot_nt(k_ref[0, :, cols], q_ref[0, :, cols])
        scores = scores + dot_nt(kr_ref[0, :, :ROPE], q_ref[0, :, rope_cols(heads, head)])
        scores = jnp.where(allowed, scores * scale, MASKED)
        top = jnp.max(scores, axis=0, keepdims=True)
        weights = jnp.exp(scores - top)
        total = jnp.sum(weights, axis=0, keepdims=True)
        lse_ref[0, head : head + 1, :] = top + jnp.log(total)
        probs = (weights * (1.0 / total)).astype(BF16)
        o_ref[0, :, cols] = dot_tn(probs, v_ref[0, :, cols]).astype(BF16)


def backward_kernel(
    heads,
    scale,
    q_ref,
    k_ref,
    v_ref,
    kr_ref,
    do_ref,
    lse_ref,
    pq_ref,
    pk_ref,
    turn_ref,
    dq_ref,
    dkv_ref,
    dkr_ref,
    dkv_acc,
    dkr_acc,
):
    step = pl.program_id(1)

    @pl.when(step == 0)
    def _():
        dkv_acc[...] = jnp.zeros_like(dkv_acc)
        dkr_acc[...] = jnp.zeros_like(dkr_acc)

    allowed = pk_ref[0] <= pq_ref[0]
    pieces = []
    for head in range(heads):
        cols = head_cols(head)
        value_cols = head_cols(heads + head)
        keys = k_ref[0, :, cols]
        query = q_ref[0, :, cols]
        query_rope = q_ref[0, :, rope_cols(heads, head)]
        grad = do_ref[0, :, cols]
        scores = dot_nt(keys, query) + dot_nt(kr_ref[0, :, :ROPE], query_rope)
        probs = jnp.where(
            allowed, jnp.exp(scores * scale - lse_ref[0, head : head + 1, :]), 0.0
        )
        grad_probs = dot_nt(v_ref[0, :, cols], grad)
        inner = jnp.sum(probs * grad_probs, axis=0, keepdims=True)
        grad_raw = (probs * (grad_probs - inner) * scale).astype(BF16)
        dkv_acc[:, value_cols] += dot_nn(probs.astype(BF16), grad)
        dkv_acc[:, cols] += dot_nn(grad_raw, query)
        dkr_acc[...] += dot_nn(grad_raw, query_rope)
        turned = dot_tn(grad_raw, kr_ref[0]) * turn_ref[0]
        pieces.append(dot_tn(grad_raw, keys))
        pieces.append(turned[:, :ROPE] + turned[:, ROPE:])
    dq_ref[0] = jnp.concatenate(pieces, axis=1).astype(BF16)

    @pl.when(step == pl.num_programs(1) - 1)
    def _():
        dkv_ref[0] = dkv_acc[...].astype(BF16)
        dkr_ref[0] = dkr_acc[...].astype(BF16)


def query_tile(rows, total_rows):
    return min(rows, max(128, 256 * 1024 // total_rows))


def attend(queries, pairs, key_rope, pos_q, pos_k, heads, scale):
    seqs, rows, width = queries.shape
    total_rows = pairs.shape[1]
    tile = query_tile(rows, total_rows)
    flat = heads * NOPE
    return pl.pallas_call(
        functools.partial(forward_kernel, heads, scale),
        grid=(seqs, rows // tile),
        in_specs=[
            pl.BlockSpec((1, tile, width), lambda s, i: (s, i, 0)),
            pl.BlockSpec((1, total_rows, flat), lambda s, i: (s, 0, 0)),
            pl.BlockSpec((1, total_rows, flat), lambda s, i: (s, 0, 1)),
            pl.BlockSpec((1, total_rows, 2 * ROPE), lambda s, i: (s, 0, LATENT // (2 * ROPE))),
            pl.BlockSpec((1, 1, tile), lambda s, i: (s, 0, i)),
            pl.BlockSpec((1, total_rows, 1), lambda s, i: (s, 0, 0)),
        ],
        out_specs=[
            pl.BlockSpec((1, tile, flat), lambda s, i: (s, i, 0)),
            pl.BlockSpec((1, heads, tile), lambda s, i: (s, 0, i)),
        ],
        out_shape=[
            jax.ShapeDtypeStruct((seqs, rows, flat), BF16),
            jax.ShapeDtypeStruct((seqs, heads, rows), F32),
        ],
        cost_estimate=pl.CostEstimate(
            flops=2 * seqs * heads * rows * total_rows * (NOPE + ROPE + VDIM),
            transcendentals=seqs * heads * rows * total_rows,
            bytes_accessed=2 * seqs * (rows * width + 2 * total_rows * flat),
        ),
    )(queries, pairs, pairs, key_rope, pos_q[:, None, :], pos_k[:, :, None])


def attend_back(queries, pairs, key_rope, grads, lse, pos_q, pos_k, turns, heads, scale):
    seqs, rows, width = queries.shape
    total_rows = pairs.shape[1]
    tile = query_tile(rows, total_rows)
    flat = heads * NOPE
    whole = lambda s, i: (s, 0, 0)
    piece = lambda s, i: (s, i, 0)
    return pl.pallas_call(
        functools.partial(backward_kernel, heads, scale),
        grid=(seqs, rows // tile),
        in_specs=[
            pl.BlockSpec((1, tile, width), piece),
            pl.BlockSpec((1, total_rows, flat), whole),
            pl.BlockSpec((1, total_rows, flat), lambda s, i: (s, 0, 1)),
            pl.BlockSpec((1, total_rows, 2 * ROPE), lambda s, i: (s, 0, LATENT // (2 * ROPE))),
            pl.BlockSpec((1, tile, flat), piece),
            pl.BlockSpec((1, heads, tile), lambda s, i: (s, 0, i)),
            pl.BlockSpec((1, 1, tile), lambda s, i: (s, 0, i)),
            pl.BlockSpec((1, total_rows, 1), whole),
            pl.BlockSpec((1, tile, 2 * ROPE), piece),
        ],
        out_specs=[
            pl.BlockSpec((1, tile, width), piece),
            pl.BlockSpec((1, total_rows, 2 * flat), whole),
            pl.BlockSpec((1, total_rows, ROPE), whole),
        ],
        out_shape=[
            jax.ShapeDtypeStruct((seqs, rows, width), BF16),
            jax.ShapeDtypeStruct((seqs, total_rows, 2 * flat), BF16),
            jax.ShapeDtypeStruct((seqs, total_rows, ROPE), BF16),
        ],
        scratch_shapes=[
            pltpu.VMEM((total_rows, 2 * flat), F32),
            pltpu.VMEM((total_rows, ROPE), F32),
        ],
        cost_estimate=pl.CostEstimate(
            flops=4 * seqs * heads * rows * total_rows * (NOPE + ROPE + VDIM),
            transcendentals=seqs * heads * rows * total_rows,
            bytes_accessed=2 * seqs * (rows * width + 4 * total_rows * flat),
        ),
    )(
        queries, pairs, pairs, key_rope, grads, lse, pos_q[:, None, :], pos_k[:, :, None], turns
    )


def join_kernel(count, *refs):
    rows = refs[0].shape[1]
    for j in range(count):
        refs[count][0, j * rows : (j + 1) * rows, :] = refs[j][0]


def join_norm_kernel(count, width, *refs):
    gain, out, tail = refs[count][...], refs[count + 1], refs[count + 2]
    rows = refs[0].shape[1]
    for j in range(count):
        values = refs[j][0, :, :width].astype(F32)
        inverse = lax.rsqrt(jnp.mean(values * values, axis=-1, keepdims=True) + EPSILON)
        part = slice(j * rows, (j + 1) * rows)
        out[0, part, :] = (values * inverse * gain).astype(BF16)
        tail[0, part, :] = refs[j][0, :, width:]


def join_norm(blocks, gain):
    seqs, rows, total = blocks[0].shape
    width = gain.shape[0]
    count = len(blocks)
    first = lambda s: (s, 0, 0)
    return pl.pallas_call(
        functools.partial(join_norm_kernel, count, width),
        grid=(seqs,),
        in_specs=[pl.BlockSpec((1, rows, total), first)] * count
        + [pl.BlockSpec((1, width), lambda s: (0, 0))],
        out_specs=[
            pl.BlockSpec((1, count * rows, width), first),
            pl.BlockSpec((1, count * rows, total - width), first),
        ],
        out_shape=[
            jax.ShapeDtypeStruct((seqs, count * rows, width), BF16),
            jax.ShapeDtypeStruct((seqs, count * rows, total - width), BF16),
        ],
        cost_estimate=pl.CostEstimate(
            flops=0, transcendentals=0, bytes_accessed=4 * seqs * count * rows * total
        ),
    )(*blocks, gain[None])


def join(blocks):
    seqs, rows, width = blocks[0].shape
    count = len(blocks)
    return pl.pallas_call(
        functools.partial(join_kernel, count),
        grid=(seqs,),
        in_specs=[pl.BlockSpec((1, rows, width), lambda s: (s, 0, 0))] * count,
        out_specs=pl.BlockSpec((1, count * rows, width), lambda s: (s, 0, 0)),
        out_shape=jax.ShapeDtypeStruct((seqs, count * rows, width), BF16),
        cost_estimate=pl.CostEstimate(
            flops=0, transcendentals=0, bytes_accessed=4 * seqs * count * rows * width
        ),
    )(*blocks)


def pick_kernel(count, slots, *refs):
    near, far = refs[count + 2], refs[count + 3]
    for j in range(count):
        rows = refs[j][0]
        part = slice(j * slots, (j + 1) * slots)
        near[0, part, :] = dot_nn(refs[count][0, part, :], rows).astype(BF16)
        far[0, part, :] = dot_nn(refs[count + 1][0, part, :], rows).astype(BF16)


def pick_blocks(blocks, near, far):
    seqs, rows, width = blocks[0].shape
    count = len(blocks)
    total = near.shape[1]
    block = pl.BlockSpec((1, rows, width), lambda s: (s, 0, 0))
    table = pl.BlockSpec((1, total, rows), lambda s: (s, 0, 0))
    out = pl.BlockSpec((1, total, width), lambda s: (s, 0, 0))
    return pl.pallas_call(
        functools.partial(pick_kernel, count, total // count),
        grid=(seqs,),
        in_specs=[block] * count + [table] * 2,
        out_specs=[out] * 2,
        out_shape=[jax.ShapeDtypeStruct((seqs, total, width), BF16)] * 2,
        cost_estimate=pl.CostEstimate(
            flops=4 * seqs * total * rows * width,
            transcendentals=0,
            bytes_accessed=2 * seqs * (count * rows + 2 * total) * width,
        ),
    )(*blocks, near, far)


def pick_span_kernel(count, slots, rows_ref, tail_ref, near_ref, far_ref, near, far):
    piece = rows_ref.shape[1] // count
    width = rows_ref.shape[2]
    for j in range(count):
        own = slice(j * piece, (j + 1) * piece)
        part = slice(j * slots, (j + 1) * slots)
        for table, out in ((near_ref, near), (far_ref, far)):
            picks = table[0, part, :]
            out[0, part, :width] = dot_nn(picks, rows_ref[0, own, :]).astype(BF16)
            out[0, part, width:] = dot_nn(picks, tail_ref[0, own, :]).astype(BF16)


def pick_span(span_rows, tail, side, near, far):
    seqs, total, piece = near.shape
    width, extra = span_rows.shape[2], tail.shape[2]
    count = span_rows.shape[1] // (2 * piece)
    half = lambda s: (s, side, 0)
    table = pl.BlockSpec((1, total, piece), lambda s: (s, 0, 0))
    out = pl.BlockSpec((1, total, width + extra), lambda s: (s, 0, 0))
    return pl.pallas_call(
        functools.partial(pick_span_kernel, count, total // count),
        grid=(seqs,),
        in_specs=[
            pl.BlockSpec((1, count * piece, width), half),
            pl.BlockSpec((1, count * piece, extra), half),
            table,
            table,
        ],
        out_specs=[out] * 2,
        out_shape=[jax.ShapeDtypeStruct((seqs, total, width + extra), BF16)] * 2,
        cost_estimate=pl.CostEstimate(
            flops=4 * seqs * total * piece * width,
            transcendentals=0,
            bytes_accessed=2 * seqs * (count * piece + 2 * total) * width,
        ),
    )(span_rows, tail, near, far)


def place_kernel(counts, dest_ref, *refs):
    out = refs[-1]
    p = 0
    for ref, count in zip(refs, counts):
        rows = ref.shape[1] // count
        for q in range(count):
            start = pl.multiple_of(dest_ref[p] * rows, rows)
            out[0, pl.ds(start, rows), :] = ref[0, q * rows : (q + 1) * rows, :]
            p += 1


def place(arrays, dest, rows):
    seqs, _, width = arrays[0].shape
    counts = [array.shape[1] // rows for array in arrays]
    total = rows * sum(counts)
    first = lambda s, dest: (s, 0, 0)
    return pl.pallas_call(
        functools.partial(place_kernel, counts),
        grid_spec=pltpu.PrefetchScalarGridSpec(
            num_scalar_prefetch=1,
            grid=(seqs,),
            in_specs=[pl.BlockSpec((1, array.shape[1], width), first) for array in arrays],
            out_specs=pl.BlockSpec((1, total, width), first),
        ),
        out_shape=jax.ShapeDtypeStruct((seqs, total, width), BF16),
        cost_estimate=pl.CostEstimate(
            flops=0, transcendentals=0, bytes_accessed=4 * seqs * total * width
        ),
    )(dest, *arrays)


def project_kernel(count, transposed, rows_ref, weight_ref, *outs):
    dot = dot_nt if transposed else dot_nn
    result = dot(rows_ref[0], weight_ref[...]).astype(BF16)
    piece = outs[0].shape[1]
    for j in range(count):
        outs[j][0] = result[j * piece : (j + 1) * piece]


def project(span_rows, side, weight, count, transposed):
    seqs, total, depth = span_rows.shape
    group = total // 2
    width = weight.shape[0] if transposed else weight.shape[1]
    return pl.pallas_call(
        functools.partial(project_kernel, count, transposed),
        grid=(seqs,),
        in_specs=[
            pl.BlockSpec((1, group, depth), lambda s: (s, side, 0)),
            pl.BlockSpec(weight.shape, lambda s: (0, 0)),
        ],
        out_specs=[pl.BlockSpec((1, group // count, width), lambda s: (s, 0, 0))] * count,
        out_shape=[jax.ShapeDtypeStruct((seqs, group // count, width), BF16)] * count,
        cost_estimate=pl.CostEstimate(
            flops=2 * seqs * group * depth * width,
            transcendentals=0,
            bytes_accessed=2 * (seqs * group * (depth + width) + depth * width),
        ),
    )(span_rows, weight)


def spread_kernel(count, width, extra, *refs):
    base, near, near_rows, far, far_rows = refs[:5]
    outs = refs[6:] if extra else refs[5:]
    rows = outs[0].shape[1]
    slots = near.shape[1] // count
    for j in range(count):
        part = slice(j * slots, (j + 1) * slots)
        own = slice(j * rows, (j + 1) * rows)
        total = base[0, own, :].astype(F32)
        total = total + dot_tn(near[0, part, :], near_rows[0, part, :])
        total = total + dot_tn(far[0, part, :], far_rows[0, part, :])
        outs[j][0, :, :width] = total.astype(BF16)
        if extra:
            outs[j][0, :, width:] = refs[5][0, own, :]


def spread_blocks(base, side, near, near_rows, far, far_rows, columns=None):
    seqs, total, piece = near.shape
    width = base.shape[2]
    count = base.shape[1] // (2 * piece)
    group = count * piece
    first = lambda s: (s, 0, 0)
    table = pl.BlockSpec((1, total, piece), first)
    slot_rows = pl.BlockSpec((1, total, width), first)
    specs = [
        pl.BlockSpec((1, group, width), lambda s: (s, side, 0)),
        table,
        slot_rows,
        table,
        slot_rows,
    ]
    operands = [base, near, near_rows, far, far_rows]
    out_width = width
    if columns is not None:
        specs.append(pl.BlockSpec((1, group, columns.shape[2]), first))
        operands.append(columns)
        out_width = width + columns.shape[2]
    return pl.pallas_call(
        functools.partial(spread_kernel, count, width, columns is not None),
        grid=(seqs,),
        in_specs=specs,
        out_specs=[pl.BlockSpec((1, piece, out_width), first)] * count,
        out_shape=[jax.ShapeDtypeStruct((seqs, piece, out_width), BF16)] * count,
        cost_estimate=pl.CostEstimate(
            flops=4 * seqs * total * piece * width,
            transcendentals=0,
            bytes_accessed=4 * seqs * (group + total) * width,
        ),
    )(*operands)


def expert_kernel(
    top_count,
    mine_ref,
    tok_a,
    tok_b,
    raw_a,
    raw_b,
    router,
    gate_hbm,
    up_hbm,
    down_hbm,
    x_out,
    dy_out,
    hid_out,
    dgate_out,
    dup_out,
    dx_a,
    dx_b,
    out_a,
    out_b,
    dg_out,
    w_gate,
    w_up,
    w_down,
    gates,
    sems,
):
    half, width = tok_a.shape
    hidden = w_gate.shape[1]
    tile = 256
    spans = [(f, min(tile, hidden - f)) for f in range(0, hidden, tile)]

    def copies(i, start, size):
        cols = pl.ds(start, size)
        return (
            pltpu.make_async_copy(gate_hbm.at[0, :, cols], w_gate.at[:, cols], sems.at[0, i]),
            pltpu.make_async_copy(up_hbm.at[0, :, cols], w_up.at[:, cols], sems.at[1, i]),
            pltpu.make_async_copy(down_hbm.at[0, cols, :], w_down.at[cols, :], sems.at[2, i]),
        )

    for i, (start, size) in enumerate(spans):
        for copy in copies(i, start, size):
            copy.start()
    mine = mine_ref[0].astype(F32)
    for part, (tok, raw) in enumerate(((tok_a, raw_a), (tok_b, raw_b))):
        rows = slice(part * half, (part + 1) * half)
        x_out[rows, :] = tok[...]
        logits = dot_nt(tok[...], router[...])
        experts = lax.broadcasted_iota(jnp.int32, logits.shape, 1).astype(F32)
        named = raw[:, width:].astype(F32)
        routes = [named[:, j : j + 1] for j in range(top_count)]
        chosen = [
            jnp.sum(jnp.where(experts == r, logits, 0.0), axis=-1, keepdims=True) for r in routes
        ]
        best = functools.reduce(jnp.maximum, chosen)
        powers = [jnp.exp(c - best) for c in chosen]
        wanted = sum(jnp.where(r == mine, p, 0.0) for r, p in zip(routes, powers))
        gate = wanted / sum(powers)
        gates[rows, :] = gate
        dy_out[rows, :] = (raw[:, :width].astype(F32) * gate).astype(BF16)

    def hidden_part(i, start, size):
        for copy in copies(i, start, size):
            copy.wait()
        cols = pl.ds(start, size)
        gate = dot_nn(x_out[...], w_gate[:, cols])
        upward = dot_nn(x_out[...], w_up[:, cols])
        grad = dot_nt(dy_out[...], w_down[cols, :])
        sigmoid = 1.0 / (1.0 + jnp.exp(-gate))
        passed = gate * sigmoid
        hid_out[:, cols] = (passed * upward).astype(BF16)
        dgate_out[:, cols] = (
            grad * upward * sigmoid * (1.0 + gate * (1.0 - sigmoid))
        ).astype(BF16)
        dup_out[:, cols] = (grad * passed).astype(BF16)

    full = hidden // tile

    @pl.loop(0, full)
    def _(i):
        hidden_part(i, pl.multiple_of(i * tile, tile), tile)

    if full < len(spans):
        hidden_part(full, *spans[full])

    def width_part(n, dg):
        cols = pl.ds(pl.multiple_of(n * tile, tile), tile)
        result = dot_nn(hid_out[...], w_down[:, cols])
        grad = dot_nt(dgate_out[...], w_gate[cols, :]) + dot_nt(dup_out[...], w_up[cols, :])
        dx_a[:, cols] = grad[:half].astype(BF16)
        dx_b[:, cols] = grad[half:].astype(BF16)
        scaled = (result * gates[...]).astype(BF16)
        out_a[:, cols] = scaled[:half]
        out_b[:, cols] = scaled[half:]
        raw = jnp.concatenate([raw_a[:, cols], raw_b[:, cols]], axis=0).astype(F32)
        return dg + jnp.sum(raw * result, axis=-1, keepdims=True)

    dg_out[...] = lax.fori_loop(0, width // tile, width_part, jnp.zeros((2 * half, 1), F32))


def expert_rows(mine, tokens, grads, router, w_gate, w_up, w_down):
    half, width = tokens[0].shape
    hidden = w_gate.shape[2]
    rows = 2 * half
    parts = -(-hidden // 256)
    vmem = pl.BlockSpec(memory_space=pltpu.VMEM)
    shapes = [(rows, width)] * 2 + [(rows, hidden)] * 3 + [(half, width)] * 4
    return pl.pallas_call(
        functools.partial(expert_kernel, TOP),
        in_specs=[pl.BlockSpec(memory_space=pltpu.SMEM)]
        + [vmem] * 5
        + [pl.BlockSpec(memory_space=pl.ANY)] * 3,
        out_specs=[vmem] * 10,
        out_shape=[jax.ShapeDtypeStruct(shape, BF16) for shape in shapes]
        + [jax.ShapeDtypeStruct((rows, 1), F32)],
        scratch_shapes=[
            pltpu.VMEM((width, hidden), BF16),
            pltpu.VMEM((width, hidden), BF16),
            pltpu.VMEM((hidden, width), BF16),
            pltpu.VMEM((rows, 1), F32),
            pltpu.SemaphoreType.DMA((3, parts)),
        ],
        compiler_params=pltpu.CompilerParams(vmem_limit_bytes=60 * 1024 * 1024),
        cost_estimate=pl.CostEstimate(
            flops=12 * rows * width * hidden,
            transcendentals=rows * hidden,
            bytes_accessed=2 * (3 * width * hidden + 8 * rows * width + 3 * rows * hidden),
        ),
    )(mine, *tokens, *grads, router, w_gate, w_up, w_down)


def half_kernel(half_ref, far_in, near_in, *refs):
    count = 1
    fars, nears = refs[:count], refs[count : 2 * count]
    outs = refs[-count:]
    for j in range(count):
        total = dot_tn(far_in[...], fars[j][...]) + dot_tn(near_in[...], nears[j][...])
        if len(refs) > 3 * count:
            total = total + refs[2 * count + j][...].astype(F32)
        outs[j][...] = total.astype(outs[j].dtype)


def half_grads(far_in, near_in, far_grad, near_grad, half, received=None):
    depth, width = far_in.shape
    columns = far_grad.shape[1]
    tile = 512
    steps = width // 2 // tile
    taken = pl.BlockSpec((depth, tile), lambda i, half: (0, half[0] * steps + i))
    whole = pl.BlockSpec((depth, columns), lambda i, half: (0, 0))
    out = pl.BlockSpec((tile, columns), lambda i, half: (i, 0))
    operands = [far_in, near_in, far_grad, near_grad]
    specs = [taken] * 2 + [whole] * 2
    kind = BF16
    if received is not None:
        operands.append(received)
        specs.append(out)
        kind = F32
    return pl.pallas_call(
        half_kernel,
        grid_spec=pltpu.PrefetchScalarGridSpec(
            num_scalar_prefetch=1, grid=(steps,), in_specs=specs, out_specs=[out]
        ),
        out_shape=[jax.ShapeDtypeStruct((width // 2, columns), kind)],
        cost_estimate=pl.CostEstimate(
            flops=2 * depth * width * columns,
            transcendentals=0,
            bytes_accessed=2 * (depth * width + 2 * depth * columns + width * columns),
        ),
    )(half, *operands)[0]


def down_kernel(rank_ref, far_in, near_in, far_grad, near_grad, theirs, mine, total):
    half = theirs.shape[0]
    total[...] = dot_tn(far_in[...], far_grad[...]) + dot_tn(near_in[...], near_grad[...])
    rank = rank_ref[0]
    theirs[...] = total[pl.ds(pl.multiple_of((1 - rank) * half, 8), half), :].astype(BF16)
    mine[...] = total[pl.ds(pl.multiple_of(rank * half, 8), half), :].astype(BF16)


def down_grads(far_in, near_in, far_grad, near_grad, rank, side):
    depth, rows = far_in.shape
    width = far_grad.shape[1] // 2
    tile = 1024
    whole = pl.BlockSpec((depth, rows), lambda i, rank: (0, 0))
    piece = pl.BlockSpec((depth, tile), lambda i, rank: (0, side * (width // tile) + i))
    out = pl.BlockSpec((rows // 2, tile), lambda i, rank: (0, i))
    return pl.pallas_call(
        down_kernel,
        grid_spec=pltpu.PrefetchScalarGridSpec(
            num_scalar_prefetch=1,
            grid=(width // tile,),
            in_specs=[whole] * 2 + [piece] * 2,
            out_specs=[out] * 2,
            scratch_shapes=[pltpu.VMEM((rows, tile), F32)],
        ),
        out_shape=[jax.ShapeDtypeStruct((rows // 2, width), BF16)] * 2,
        cost_estimate=pl.CostEstimate(
            flops=4 * depth * rows * width,
            transcendentals=0,
            bytes_accessed=4 * depth * (rows + width) + 2 * rows * width,
        ),
    )(rank, far_in, near_in, far_grad, near_grad)


def merge_kernel(mine_a, mine_b, got_a, got_b, out):
    half = mine_a.shape[1]
    for j, (mine, got) in enumerate(((mine_a, got_a), (mine_b, got_b))):
        total = mine[...].astype(F32) + got[...].astype(F32)
        out[:, j * half : (j + 1) * half] = total


def merge_down(*parts):
    rows, half = parts[0].shape
    tile = rows // 4
    return pl.pallas_call(
        merge_kernel,
        grid=(4,),
        in_specs=[pl.BlockSpec((tile, half), lambda i: (i, 0))] * 4,
        out_specs=pl.BlockSpec((tile, 2 * half), lambda i: (i, 0)),
        out_shape=jax.ShapeDtypeStruct((rows, 2 * half), F32),
        cost_estimate=pl.CostEstimate(
            flops=0, transcendentals=0, bytes_accessed=16 * rows * half
        ),
    )(*parts)


def after(value, *others):
    return lax.optimization_barrier((value, *others))[0]


def layer(
    hidden_in,
    out_grad,
    routes,
    block_order,
    norm_attn,
    w_query,
    w_kv_down,
    norm_latent,
    w_key_up,
    w_value_up,
    w_out,
    norm_ffn,
    w_router,
    shared_gate,
    shared_up,
    shared_down,
    expert_gate,
    expert_up,
    expert_down,
):
    seqs, piece, width = hidden_in.shape
    n_expert = lax.axis_size(EXPERT)
    n_ctx = lax.axis_size(CTX)
    n_dp = lax.axis_size(DP)
    lanes = n_expert // 2
    heads = w_query.shape[1] // (NOPE + ROPE)
    expert_count = w_router.shape[1]
    slots = 8 * ((piece * TOP + 6 * expert_count - 1) // (6 * expert_count))
    expert_rank = lax.axis_index(EXPERT)
    ctx_rank = lax.axis_index(CTX)
    dp_rank = lax.axis_index(DP)
    span = piece * n_expert
    total_rows = span * n_ctx
    scale = (NOPE + ROPE) ** (-0.5)
    group = lanes * piece
    group_slots = lanes * slots

    def shift(value, steps):
        pairs = [(e, (e + 2 * steps) % n_expert) for e in range(n_expert)]
        return lax.ppermute(value, EXPERT, pairs)

    def across(value):
        return lax.ppermute(value, EXPERT, [(e, e ^ 1) for e in range(n_expert)])

    def other_dp(value):
        return lax.ppermute(value, DP, [(d, n_dp - 1 - d) for d in range(n_dp)])

    def other_ctx(value):
        return lax.ppermute(value, CTX, [(c, n_ctx - 1 - c) for c in range(n_ctx)])

    up_count = lanes // 2
    down_count = lanes - 1 - up_count

    def gather_blocks(own):
        ups, downs = [own], [own]
        for k in range(max(up_count, down_count)):
            if k < up_count:
                ups.append(shift(ups[-1], 1))
            if k < down_count:
                downs.append(shift(downs[-1], -1))
        column = ups + downs[:0:-1]
        return column + [across(b) for b in column]

    def gather_ctx(value):
        if n_ctx == 2:
            return [value, other_ctx(value)], [ctx_rank, 1 - ctx_rank]
        return [lax.all_gather(value, CTX, axis=1, tiled=True)], list(range(n_ctx))

    def scatter_ctx(value):
        if n_ctx == 2:
            half = value.shape[1] // 2
            return add(value[:, :half], other_ctx(value[:, half:]))
        return lax.psum_scatter(value, CTX, scatter_dimension=1, tiled=True)

    def add(*terms):
        total = terms[0].astype(F32)
        for term in terms[1:]:
            total = total + term.astype(F32)
        return total.astype(BF16)

    def scatter_blocks(part, hold=()):
        order = [up_count] + [k for k in range(lanes - 1, 0, -1) if k != up_count] + [0]
        crossed = {k: across(part(lanes + k)) for k in order}
        sums = {k: (part(k), crossed[k]) for k in order}
        marks = [crossed[up_count]]
        moving = add(*sums[up_count])
        for k in range(up_count, 0, -1):
            if k == 1 and hold:
                moving = after(moving, *hold)
            moving = shift(moving, -1)
            marks.append(moving)
            if k > 1:
                moving = add(*sums[k - 1], moving)
        result = [*sums[0], moving]
        if down_count:
            moving = add(*sums[lanes - down_count])
            for d in range(down_count, 0, -1):
                moving = shift(moving, 1)
                if d > 1:
                    moving = add(*sums[lanes - d + 1], moving)
            result.append(moving)
        return sum(term.astype(F32) for term in result), marks

    def sum_copies(grad, small=False):
        sent = grad.astype(BF16)
        if n_ctx != 2:
            return lax.psum(sent, (DP, CTX)).astype(F32)
        if small:
            pair = add(sent, other_ctx(sent))
            return pair.astype(F32) + other_dp(pair).astype(F32)
        half = grad.shape[0] // 2
        mine = lax.dynamic_slice_in_dim(sent, ctx_rank * half, half, 0)
        theirs = lax.dynamic_slice_in_dim(sent, (1 - ctx_rank) * half, half, 0)
        pair = add(mine, other_ctx(theirs))
        full = add(pair, other_dp(pair))
        rest = other_ctx(full)
        first = ctx_rank == 0
        return jnp.concatenate(
            [jnp.where(first, full, rest), jnp.where(first, rest, full)], axis=0
        ).astype(F32)

    def split_copies(grad):
        return lax.psum_scatter(
            grad.astype(BF16), CTX, scatter_dimension=0, tiled=True
        ).astype(F32)

    rank_z, rank_x = expert_rank // 2, expert_rank % 2
    owners = [
        ((rank_z - j % lanes) % lanes) * 2 + (rank_x + j // lanes) % 2 for j in range(n_expert)
    ]
    owner_ids = jnp.stack(owners)
    ids = jnp.arange(n_expert, dtype=jnp.int32)
    block_of = ((ids % 2 + rank_x) % 2) * lanes + (rank_z - ids // 2) % lanes

    tail = 2 * ROPE
    routes_tail = jnp.pad(routes.astype(BF16), ((0, 0), (0, 0), (0, tail - TOP)))
    blocks = gather_blocks(jnp.concatenate([hidden_in, routes_tail], axis=-1))

    kv_rows = w_kv_down.shape[0]
    kv_piece = kv_rows // n_ctx
    kv_own = lax.dynamic_slice_in_dim(w_kv_down, ctx_rank * kv_piece, kv_piece, 0)
    kv_blocks = gather_blocks(kv_own)
    kv_span = join([b[None] for b in kv_blocks])
    kv_all, ctx_ranks = gather_ctx(kv_span)
    ctx_ranks = jnp.stack([jnp.asarray(r, jnp.int32) for r in ctx_ranks])
    kv_dest = (owner_ids[None, :] * n_ctx + ctx_ranks[:, None]).reshape(-1)
    kv_full = place(kv_all, kv_dest, kv_piece)[0]

    def rms(rows):
        return lax.rsqrt(jnp.mean(rows * rows, axis=-1, keepdims=True) + EPSILON)

    half_rows = total_rows // (2 * n_ctx)

    def positions(row_ids):
        matches = (row_ids // half_rows)[:, None] == jnp.arange(2 * n_ctx, dtype=jnp.int32)
        starts = jnp.sum(jnp.where(matches[None], block_order[:, None, :], 0), axis=2)
        return starts * half_rows + row_ids % half_rows

    piece_ids = jnp.arange(piece, dtype=jnp.int32)
    in_span = (owner_ids[:, None] * piece + piece_ids[None, :]).reshape(-1)
    span_pos = positions(ctx_rank * span + in_span)
    key_pos = positions((ctx_ranks[:, None] * span + in_span[None, :]).reshape(-1))
    tables = rope_tables(span_pos)
    span_cos, span_sin = tables
    turns = jnp.concatenate([span_cos, span_cos, span_sin, span_sin], axis=-1)
    span_cos = jnp.tile(span_cos, (1, 1, 2 * heads))
    span_sin = jnp.tile(span_sin, (1, 1, 2 * heads))

    per_head = w_query.reshape(width, heads, NOPE + ROPE)
    w_nope = per_head[..., :NOPE].reshape(width, heads * NOPE)
    w_rope = per_head[..., NOPE:]
    first, second = halves(w_rope)
    w_turned = jnp.concatenate([-second, first], axis=-1).reshape(width, heads * ROPE)
    w_inner = jnp.concatenate([w_nope, w_rope.reshape(width, heads * ROPE), w_turned], axis=-1)
    w_up = jnp.concatenate([w_key_up, w_value_up], axis=-1)
    shared_width = shared_gate.shape[1]
    shared_room = -(-shared_width // 128) * 128
    spare = ((0, shared_room - shared_width), (0, 0))
    w_shared = jnp.concatenate([jnp.pad(shared_gate.T, spare), jnp.pad(shared_up.T, spare)], axis=0)
    w_shared_down = jnp.pad(shared_down, spare)
    w_inner, w_up, w_shared, w_shared_down = lax.optimization_barrier(
        (w_inner, w_up, w_shared, w_shared_down)
    )

    own_rows = hidden_in.astype(F32)
    inv_own = rms(own_rows)
    normed_span, routes_cols = join_norm(blocks, norm_attn)
    grad_all = lax.all_gather(after(out_grad, normed_span), EXPERT, axis=1, tiled=True)
    kv_joint = product(normed_span, kv_full)
    latent_raw = kv_joint[..., :LATENT]
    inv_latent = rms(latent_raw)
    key_rope = rotate(kv_joint[..., LATENT:], tables)
    rope_first, rope_second = halves(key_rope)
    latent_span = jnp.concatenate(
        [latent_raw * inv_latent * norm_latent, key_rope, rope_second, -rope_first], axis=-1
    ).astype(BF16)
    latent_all = gather_ctx(latent_span)[0]
    latent_all = jnp.concatenate(latent_all, axis=1) if len(latent_all) > 1 else latent_all[0]
    query_raw = product(normed_span, w_inner)
    flat = heads * NOPE
    queries = jnp.concatenate(
        [
            query_raw[..., :flat],
            query_raw[..., flat : flat + heads * ROPE] * span_cos
            + query_raw[..., flat + heads * ROPE :] * span_sin,
        ],
        axis=-1,
    ).astype(BF16)
    latent_part = latent_all[..., :LATENT]
    pairs = product(latent_part, w_up).astype(BF16)
    heads_out, lse = attend(queries, pairs, latent_all, span_pos, key_pos, heads, scale)

    def block_of_span(array, j):
        return array[:, j * piece : (j + 1) * piece]

    routes_span = routes_cols[..., :TOP].astype(jnp.int32).reshape(seqs, n_expert, piece, TOP)
    mine = dp_rank * n_expert + expert_rank
    theirs = (n_dp - 1 - dp_rank) * n_expert + expert_rank
    earlier = (piece_ids[:, None] < piece_ids[None, :]).astype(F32)
    slot_ids = jnp.arange(slots, dtype=jnp.int32)
    picks = []
    for target in (mine, theirs):
        named = jnp.any(routes_span == target, axis=-1)
        rank = jnp.einsum("sjp,pq->sjq", named.astype(F32), earlier).astype(jnp.int32)
        picks.append(jnp.where(named, rank, -1)[:, :, None, :] == slot_ids[:, None])

    def side_tables(table):
        return [
            table[:, side * lanes : (side + 1) * lanes].reshape(seqs, group_slots, piece)
            for side in range(2)
        ]

    near_tables = side_tables(picks[0].astype(BF16))
    far_tables = side_tables(picks[1].astype(BF16))
    grad_span = place([grad_all], block_of, piece)
    grad_slots = [
        pick_span(grad_span, routes_cols, side, near_tables[side], far_tables[side])
        for side in range(2)
    ]
    grad_got = [other_dp(grad_slots[side][1]) for side in range(2)]
    sh_dhidden = back_product(grad_span, w_shared_down)

    def project_sides(rows, weight, transposed):
        far_side = project(rows, 1, weight, lanes, transposed)
        near_side = project(rows, 0, weight, lanes, transposed)
        return lambda j: (near_side, far_side)[j // lanes][j % lanes]

    attn_own, _ = scatter_blocks(
        project_sides(heads_out, w_out, False),
        hold=(sh_dhidden, grad_slots[0][1], grad_slots[1][1]),
    )
    residual = own_rows + attn_own
    inv_ffn = rms(residual)
    unit_ffn = residual * inv_ffn
    normed_ffn = (unit_ffn * norm_ffn).astype(BF16)
    ffn_blocks = gather_blocks(normed_ffn)
    token_slots = [
        pick_blocks(
            ffn_blocks[side * lanes : (side + 1) * lanes], near_tables[side], far_tables[side]
        )
        for side in range(2)
    ]
    token_got = [other_dp(token_slots[side][1]) for side in range(2)]
    ffn_span = join([after(b, token_slots[1][1]) for b in ffn_blocks])

    sh_both = back_product(ffn_span, w_shared)
    sh_gate, sh_up = sh_both[..., :shared_room], sh_both[..., shared_room:]
    sh_hidden = (jax.nn.silu(sh_gate) * sh_up).astype(BF16)
    sh_dboth = jnp.concatenate(silu_grads(sh_dhidden, sh_gate, sh_up), axis=-1)
    sh_dnorm = product(sh_dboth, w_shared).astype(BF16)

    slot_shape = (seqs, group_slots)

    def expert(tokens, grads):
        rows = [t.reshape(seqs * group_slots, -1) for t in (*tokens, *grads)]
        results = expert_rows(
            mine.reshape(1),
            rows[:2],
            rows[2:],
            w_router.T,
            expert_gate,
            expert_up,
            expert_down,
        )
        dx, out = [
            [side.reshape(*slot_shape, width) for side in pair]
            for pair in (results[5:7], results[7:9])
        ]
        return results[:5], dx, out, results[9].reshape(2, *slot_shape)

    far, far_dx, far_out, far_dg = expert([after(t, sh_dnorm) for t in token_got], grad_got)
    dg_back = other_dp(far_dg)
    dx_back = [None, None]
    dx_back[1] = other_dp(far_dx[1])
    dx_back[0] = other_dp(far_dx[0])
    out_back = [other_dp(after(far_out[side], *dx_back)) for side in range(2)]
    near, near_dx, near_out, near_dg = expert(
        [after(t[0], far_dx[1]) for t in token_slots], [g[0] for g in grad_slots]
    )

    lane_ids = jnp.arange(128, dtype=jnp.int32)

    def dg_columns(side):
        columns = 0.0
        for pick, dg, target in ((picks[0], near_dg, mine), (picks[1], dg_back, theirs)):
            table = pick[:, side * lanes : (side + 1) * lanes]
            values = dg[side].reshape(seqs, lanes, slots, 1)
            rows = jnp.sum(jnp.where(table, values, 0.0), axis=2).reshape(seqs, group, 1)
            top = rows.astype(BF16).astype(F32)
            columns = columns + jnp.where(lane_ids == target, top, 0.0)
            columns = columns + jnp.where(lane_ids == target + expert_count, rows - top, 0.0)
        return columns.astype(BF16)

    dnorm_blocks = [
        spread_blocks(
            sh_dnorm,
            side,
            near_tables[side],
            near_dx[side],
            far_tables[side],
            dx_back[side],
            dg_columns(side),
        )
        for side in range(2)
    ]
    dnorm_sum, marks = scatter_blocks(lambda j: dnorm_blocks[j // lanes][j % lanes])

    grad_sh_in = weight_grad(sh_dboth, ffn_span).astype(BF16)
    grad_sh_down = weight_grad(sh_hidden, grad_span).astype(BF16)
    grad_sh_in, grad_sh_down = lax.psum(
        (after(grad_sh_in, dnorm_blocks[0][0]), after(grad_sh_down, dnorm_blocks[0][0])),
        (DP, CTX),
    )

    dg_own = (
        dnorm_sum[..., width : width + expert_count]
        + dnorm_sum[..., width + expert_count : width + 2 * expert_count]
    )
    dnorm_sum = dnorm_sum[..., :width]
    route_hot = routes[..., None] == jnp.arange(expert_count, dtype=jnp.int32)
    logits = product(normed_ffn, w_router)
    chosen = jnp.sum(jnp.where(route_hot, logits[:, :, None, :], 0.0), axis=-1)
    gate_weights = jax.nn.softmax(chosen, axis=-1)
    grad_choice = jnp.sum(jnp.where(route_hot, dg_own[:, :, None, :], 0.0), axis=-1)
    grad_chosen = gate_weights * (
        grad_choice - jnp.sum(gate_weights * grad_choice, axis=-1, keepdims=True)
    )
    grad_logits = jnp.sum(jnp.where(route_hot, grad_chosen[..., None], 0.0), axis=2).astype(BF16)
    dnorm_ffn = dnorm_sum + back_product(grad_logits, w_router)
    grad_resid = out_grad.astype(F32) + norm_back(dnorm_ffn, residual, inv_ffn, norm_ffn)
    attn_blocks = gather_blocks(grad_resid.astype(BF16))
    grad_attn = join(attn_blocks)
    grad_router = weight_grad(normed_ffn, after(grad_logits, attn_blocks[1]))
    grad_gain_ffn = jnp.sum(after(dnorm_ffn, attn_blocks[1]) * unit_ffn, axis=(0, 1))

    sh_out = product(after(sh_hidden, marks[1]), w_shared_down).astype(BF16)
    out_blocks = []
    for side in range(2):
        out_blocks += spread_blocks(
            sh_out,
            side,
            near_tables[side],
            near_out[side],
            far_tables[side],
            out_back[side],
        )
    out_part = place(out_blocks, owner_ids, piece)
    out_own = lax.psum_scatter(out_part, EXPERT, scatter_dimension=1, tiled=True)
    out_hidden = (residual + out_own.astype(F32)).astype(BF16)

    if n_ctx == 2:
        rank = ctx_rank.reshape(1)
        ready = after(rank, dnorm_blocks[0][0])
        got = []
        for i in (3, 4):
            part = half_grads(far[0], near[0], far[i], near[i], 1 - ready)
            got.append(other_ctx(part))
        down_mine = []
        for side in range(2):
            part, own = down_grads(far[2], near[2], far[1], near[1], ready, side)
            got.append(other_ctx(part))
            down_mine.append(own)
    else:
        rows_in, grads_in, ex_hidden, ex_dgate, ex_dup = [
            jnp.concatenate([f, n], axis=0) for f, n in zip(far[:5], near[:5])
        ]
        exp_grads = [
            split_copies(weight_grad(rows_in, ex_dgate)),
            split_copies(weight_grad(rows_in, ex_dup)),
            split_copies(weight_grad(ex_hidden, grads_in)),
        ]

    grad_heads = back_product(grad_attn, w_out).astype(BF16)
    grad_queries, grad_pairs, grad_key_rope = attend_back(
        queries, pairs, latent_all, grad_heads, lse, span_pos, key_pos, turns, heads, scale
    )
    grad_latent = jnp.concatenate(
        [back_product(grad_pairs, w_up).astype(BF16), grad_key_rope], axis=-1
    )

    def by_rank(array):
        return array.reshape(n_expert, -1)

    def padded(array, size):
        return jnp.pad(array, ((0, 0), (0, size - array.shape[1])))

    room = seqs * piece * ROPE
    early = jnp.concatenate([by_rank(grad_gain_ffn), by_rank(grad_router)], axis=1)
    early_size = early.shape[1]
    early = jnp.take(padded(early, room).astype(BF16), owner_ids, axis=0, mode="clip")
    early = early.reshape(n_expert, seqs, piece, ROPE).transpose(1, 0, 2, 3)
    grad_latent_span = jnp.concatenate(
        [scatter_ctx(grad_latent), early.reshape(seqs, span, ROPE)], axis=-1
    )
    dnorm_own, marks = scatter_blocks(project_sides(grad_queries, w_query, True))
    grad_latent_own, lat_marks = scatter_blocks(lambda j: block_of_span(grad_latent_span, j))
    early = grad_latent_own[..., LATENT + ROPE :].reshape(-1)[:early_size]

    grad_query_part = weight_grad(normed_span, after(grad_queries, lat_marks[1]))
    grad_up_part = weight_grad(latent_part, after(grad_pairs, lat_marks[1]))
    grad_out_part = weight_grad(heads_out, grad_attn)
    grad_query_w = sum_copies(grad_query_part)
    grad_out_w = sum_copies(grad_out_part)
    grad_up = sum_copies(grad_up_part, small=True)
    if n_ctx == 2:
        exp_grads = []
        for i in range(2):
            exp_grads.append(
                half_grads(far[0], near[0], far[3 + i], near[3 + i], after(rank, marks[0]), got[i])
            )
    gain_part = jnp.sum(grad_query_part * w_query.astype(F32), axis=-1) / norm_attn
    gain_latent_part = jnp.sum(grad_up_part * w_up.astype(F32), axis=-1) / norm_latent
    late = jnp.concatenate([by_rank(gain_part), by_rank(gain_latent_part)], axis=1)
    late_size = late.shape[1]
    late = padded(late.reshape(1, -1), room).astype(BF16).reshape(seqs, piece, ROPE)

    grad_unit = grad_latent_own[..., :LATENT]
    own_tables = [table[:, :piece] for table in tables]
    grad_kv = jnp.concatenate(
        [
            norm_back(grad_unit, latent_raw[:, :piece], inv_latent[:, :piece], norm_latent),
            unrotate(grad_latent_own[..., LATENT : LATENT + ROPE], own_tables),
        ],
        axis=-1,
    ).astype(BF16)
    kv_grads = gather_blocks(jnp.concatenate([grad_kv, late], axis=-1))
    grad_kv_span = join(kv_grads)
    shared_sums = lax.optimization_barrier(
        (grad_sh_in, grad_sh_down, kv_grads[lanes + up_count])
    )[:2]
    if n_ctx == 2:
        exp_grads.append(merge_down(*down_mine, *got[2:]))
    dnorm_kv = back_product(grad_kv, kv_full)
    in_grad = (
        grad_resid + norm_back(dnorm_own + dnorm_kv, own_rows, inv_own, norm_attn)
    ).astype(BF16)
    normed_cols = lax.dynamic_slice_in_dim(normed_span, expert_rank * kv_rows, kv_rows, 2)
    late = (
        grad_kv_span[..., LATENT + ROPE :]
        .reshape(seqs, n_expert, piece, ROPE)
        .transpose(1, 0, 2, 3)
        .reshape(n_expert, -1)[:, : n_expert * late_size]
        .reshape(n_expert, n_expert, late_size)
    )
    late = jnp.sum(
        lax.dynamic_index_in_dim(late, expert_rank, 1, False).astype(F32), axis=0
    )
    rows = width // n_expert
    small = padded(jnp.concatenate([late, early])[None], kv_rows * ROPE).reshape(kv_rows, ROPE)
    kv_small = sum_copies(
        jnp.concatenate(
            [weight_grad(normed_cols, grad_kv_span[..., : LATENT + ROPE]), small], axis=-1
        ),
        small=True,
    )
    grad_kv_w = kv_small[:, : LATENT + ROPE]
    small = kv_small[:, LATENT + ROPE :].reshape(-1)
    late, early = small[:late_size], small[late_size : late_size + early_size]
    own_gain = lax.dynamic_slice_in_dim(norm_attn, expert_rank * rows, rows, 0)
    gain_kv = jnp.sum(grad_kv_w * w_kv_down.astype(F32), axis=-1) / own_gain
    return (
        out_hidden,
        in_grad,
        late[:rows] + gain_kv,
        grad_query_w,
        grad_kv_w,
        late[rows:],
        grad_up[:, :flat],
        grad_up[:, flat:],
        grad_out_w,
        early[:rows],
        early[rows:].reshape(rows, expert_count),
        shared_sums[0][:shared_width].astype(F32).T,
        shared_sums[0][shared_room : shared_room + shared_width].astype(F32).T,
        shared_sums[1][:shared_width].astype(F32),
        exp_grads[0][None],
        exp_grads[1][None],
        exp_grads[2][None],
    )


def solution(mesh):
    return jax.shard_map(
        layer,
        mesh=mesh,
        in_specs=(
            P(DP, (CTX, EXPERT), None),
            P(DP, (CTX, EXPERT), None),
            P(DP, (CTX, EXPERT), None),
            P(DP, None),
            P(),
            P(None, EXPERT),
            P(EXPERT, None),
            P(),
            P(None, EXPERT),
            P(None, EXPERT),
            P(EXPERT, None),
            P(),
            P(),
            P(None, EXPERT),
            P(None, EXPERT),
            P(EXPERT, None),
            P((DP, EXPERT), None, None),
            P((DP, EXPERT), None, None),
            P((DP, EXPERT), None, None),
        ),
        out_specs=(
            P(DP, (CTX, EXPERT), None),
            P(DP, (CTX, EXPERT), None),
            P(EXPERT),
            P(None, EXPERT),
            P(EXPERT, None),
            P(EXPERT),
            P(None, EXPERT),
            P(None, EXPERT),
            P(EXPERT, None),
            P(EXPERT),
            P(EXPERT, None),
            P(None, EXPERT),
            P(None, EXPERT),
            P(EXPERT, None),
            P((DP, EXPERT), CTX, None),
            P((DP, EXPERT), CTX, None),
            P((DP, EXPERT), CTX, None),
        ),
        check_vma=False,
    )
```

profile of v0, /device:TPU:0, one launch (start us, length us, event | category | flops | bytes accessed | tf_op | source)
XLA Modules:
  0.0 910.9 jit_solution(2239087038054006244)
XLA Ops:
  26.7 19.9 %collective-permute-done.refs_1_ = bf16[2,64,2176]{2,1,0:T(8,128)(2,1)} collective-permute-done((bf16[2,64,2176]{2,1,0:T(8,128)(2,1)S(1)}, bf16[2,64,2176]{2,1,0:T(8,128)(2,1)}, u32[]{:S(2)}, u32[]{:S(2)}) %collective-permute-start) | collective-permute-done | bytes 557088 | tf_op jit(solution)/shard_map/ppermute | solution.py:761
  57.1 8.4 collective-permute-done.8
  83.0 15.9 %collective-permute-done.6.refs_7_ = bf16[2,64,2176]{2,1,0:T(8,128)(2,1)} collective-permute-done((bf16[2,64,2176]{2,1,0:T(8,128)(2,1)S(1)}, bf16[2,64,2176]{2,1,0:T(8,128)(2,1)}, u32[]{:S(2)}, u32[]{:S(2)}) %collective-permute-start.6) | collective-permute-done | bytes 557088 | tf_op jit(solution)/shard_map/ppermute | solution.py:764
  98.9 9.3 %collective-permute-done.5.refs_6_ = bf16[2,64,2176]{2,1,0:T(8,128)(2,1)} collective-permute-done((bf16[2,64,2176]{2,1,0:T(8,128)(2,1)S(1)}, bf16[2,64,2176]{2,1,0:T(8,128)(2,1)}, u32[]{:S(2)}, u32[]{:S(2)}) %collective-permute-start.5) | collective-permute-done | bytes 557088 | tf_op jit(solution)/shard_map/ppermute | solution.py:764
  156.0 12.7 %shard_map.317 = (bf16[2,512,256]{2,1,0:T(8,128)(2,1)}, f32[2,2,512]{2,1,0:T(2,128)}) custom-call(bf16[2,512,384]{2,1,0:T(8,128)(2,1)} %pad_maximum_fusion.6.q_ref, bf16[2,1024,512]{2,1,0:T(8,128)(2,1)} %convolution_convert_fusion.3.k_ref.v_ref, bf16[2,1024,512]{2,1,0:T(8,128)(2,1)} %convolution_convert_fusion.3.k_ref.v_ref, ...), custom_call_target="tpu_custom_call" | custom-call | flops 1342177280 | bytes 2883584 | tf_op jit(solution)/shard_map/pallas_call | solution.py:184
  178.3 8.6 collective-permute-done.18
  193.3 16.0 %collective-permute-done.21 = bf16[2,64,2048]{2,1,0:T(8,128)(2,1)S(1)} collective-permute-done((bf16[2,64,2048]{2,1,0:T(8,128)(2,1)}, bf16[2,64,2048]{2,1,0:T(8,128)(2,1)S(1)}, u32[]{:S(2)}, u32[]{:S(2)}) %collective-permute-start.21) | collective-permute-done | bytes 524320 | tf_op jit(solution)/shard_map/ppermute | solution.py:764
  231.7 9.0 collective-permute-done.20
  247.1 12.7 %collective-permute-done.24.refs_1_ = bf16[2,64,2048]{2,1,0:T(8,128)(2,1)S(1)} collective-permute-done((bf16[2,64,2048]{2,1,0:T(8,128)(2,1)S(1)}, bf16[2,64,2048]{2,1,0:T(8,128)(2,1)S(1)}, u32[]{:S(2)}, u32[]{:S(2)}) %collective-permute-start.24) | collective-permute-done | bytes 524320 | tf_op jit(solution)/shard_map/ppermute | solution.py:761
  269.4 9.6 %collective-permute-done.26.refs_2_ = bf16[2,64,2048]{2,1,0:T(8,128)(2,1)} collective-permute-done((bf16[2,64,2048]{2,1,0:T(8,128)(2,1)S(1)}, bf16[2,64,2048]{2,1,0:T(8,128)(2,1)}, u32[]{:S(2)}, u32[]{:S(2)}) %collective-permute-start.26) | collective-permute-done | bytes 524320 | tf_op jit(solution)/shard_map/ppermute | solution.py:761
  286.7 9.4 %collective-permute-done.29.refs_3_.refs_7_ = bf16[2,64,2048]{2,1,0:T(8,128)(2,1)} collective-permute-done((bf16[2,64,2048]{2,1,0:T(8,128)(2,1)}, bf16[2,64,2048]{2,1,0:T(8,128)(2,1)}, u32[]{:S(2)}, u32[]{:S(2)}) %collective-permute-start.29) | collective-permute-done | bytes 524320 | tf_op jit(solution)/shard_map/ppermute | solution.py:764
  323.4 31.9 %collective-permute-done.30 = bf16[2,128,2048]{2,1,0:T(8,128)(2,1)} collective-permute-done((bf16[2,128,2048]{2,1,0:T(8,128)(2,1)}, bf16[2,128,2048]{2,1,0:T(8,128)(2,1)}, u32[]{:S(2)}, u32[]{:S(2)}) %collective-permute-start.30) | collective-permute-done | bytes 1048608 | tf_op jit(solution)/shard_map/ppermute | solution.py:767
  355.3 16.1 %collective-permute-done.31 = bf16[2,128,2048]{2,1,0:T(8,128)(2,1)S(1)} collective-permute-done((bf16[2,128,2048]{2,1,0:T(8,128)(2,1)}, bf16[2,128,2048]{2,1,0:T(8,128)(2,1)S(1)}, u32[]{:S(2)}, u32[]{:S(2)}) %collective-permute-start.31) | collective-permute-done | bytes 1048608 | tf_op jit(solution)/shard_map/ppermute | solution.py:767
  372.4 30.6 %shard_map.326 = (bf16[512,2048]{1,0:T(8,128)(2,1)}, bf16[512,2048]{1,0:T(8,128)(2,1)}, bf16[512,1408]{1,0:T(8,128)(2,1)}, bf16[512,1408]{1,0:T(8,128)(2,1)}, bf...) custom-call(s32[1]{0:T(128)} %bitcast.39.mine_ref, ...), custom_call_target="tpu_custom_call" | custom-call | flops 17716740096 | bytes 38404096 | tf_op jit(solution)/shard_map/pallas_call | solution.py:598
  407.8 30.6 %shard_map.327 = (bf16[512,2048]{1,0:T(8,128)(2,1)}, bf16[512,2048]{1,0:T(8,128)(2,1)}, bf16[512,1408]{1,0:T(8,128)(2,1)}, bf16[512,1408]{1,0:T(8,128)(2,1)}, bf...) custom-call(s32[1]{0:T(128)} %bitcast.39.mine_ref, ...), custom_call_target="tpu_custom_call" | custom-call | flops 17716740096 | bytes 38404096 | tf_op jit(solution)/shard_map/pallas_call | solution.py:598
  466.2 26.0 %collective-permute-done.44 = bf16[2,64,2176]{2,1,0:T(8,128)(2,1)} collective-permute-done((bf16[2,64,2176]{2,1,0:T(8,128)(2,1)}, bf16[2,64,2176]{2,1,0:T(8,128)(2,1)}, u32[]{:S(2)}, u32[]{:S(2)}) %collective-permute-start.44) | collective-permute-done | bytes 557088 | tf_op jit(solution)/shard_map/ppermute | solution.py:764
  540.1 42.8 %collective-permute-done.40.refs_4_ = bf16[2,128,2048]{2,1,0:T(8,128)(2,1)} collective-permute-done((bf16[2,128,2048]{2,1,0:T(8,128)(2,1)}, bf16[2,128,2048]{2,1,0:T(8,128)(2,1)}, u32[]{:S(2)}, u32[]{:S(2)}) %collective-permute-start.40) | collective-permute-done | bytes 1048608 | tf_op jit(solution)/shard_map/ppermute | solution.py:767
  623.9 27.6 %collective-permute-done.52.refs_7_ = bf16[2,64,2048]{2,1,0:T(8,128)(2,1)} collective-permute-done((bf16[2,64,2048]{2,1,0:T(8,128)(2,1)}, bf16[2,64,2048]{2,1,0:T(8,128)(2,1)}, u32[]{:S(2)}, u32[]{:S(2)}) %collective-permute-start.52) | collective-permute-done | bytes 524320 | tf_op jit(solution)/shard_map/ppermute | solution.py:764
  651.5 13.2 %collective-permute-done.51.refs_6_ = bf16[2,64,2048]{2,1,0:T(8,128)(2,1)} collective-permute-done((bf16[2,64,2048]{2,1,0:T(8,128)(2,1)}, bf16[2,64,2048]{2,1,0:T(8,128)(2,1)}, u32[]{:S(2)}, u32[]{:S(2)}) %collective-permute-start.51) | collective-permute-done | bytes 524320 | tf_op jit(solution)/shard_map/ppermute | solution.py:764
  676.0 15.9 %shard_map.334 = (bf16[2,512,384]{2,1,0:T(8,128)(2,1)}, bf16[2,1024,512]{2,1,0:T(8,128)(2,1)}, bf16[2,1024,64]{2,1,0:T(8,128)(2,1)}) custom-call(bf16[2,512,384]{2,1,0:T(8,128)(2,1)} %pad_maximum_fusion.6.q_ref, bf16[2,1024,512]{2,1,0:T(8,128)(2,1)} %convolution_convert_fusion.3.k_ref.v_ref, bf16[2,1024,512]{2,1,0:T(8,128)(2,1)} %convolution_convert_fusion.3.k_ref.v_ref, ...), custom_call_target="tpu_custom_call" | custom-call | flops 2684354560 | bytes 4980736 | tf_op jit(solution)/shard_map/pallas_call | solution.py:218
  708.3 8.3 collective-permute-done.55
  720.8 8.1 shard_map.339
  732.6 10.4 %collective-permute-done.58 = bf16[2,64,2048]{2,1,0:T(8,128)(2,1)} collective-permute-done((bf16[2,64,2048]{2,1,0:T(8,128)(2,1)}, bf16[2,64,2048]{2,1,0:T(8,128)(2,1)}, u32[]{:S(2)}, u32[]{:S(2)}) %collective-permute-start.58) | collective-permute-done | bytes 524320 | tf_op jit(solution)/shard_map/ppermute | solution.py:764
  860.2 19.1 %collective-permute-done.76 = bf16[256,640]{0,1:T(8,128)(2,1)} collective-permute-done((bf16[256,640]{0,1:T(8,128)(2,1)}, bf16[256,640]{0,1:T(8,128)(2,1)}, u32[]{:S(2)}, u32[]{:S(2)}) %collective-permute-start.76) | collective-permute-done | bytes 327712 | tf_op jit(solution)/shard_map/ppermute | solution.py:767
  (590 shorter events, 483.5 us)
Async XLA Ops:
  7.2 204.8 %all-gather.2.cloned.1.call-start = ((), (), s32[]{:S(2)}) async-start(), calls=%async_computation.1 | async-start | bytes 4718592 | tf_op jit(solution)/shard_map/all_gather | solution.py:909
  8.3 40.5 %collective-permute-start.10 = (bf16[128,576]{1,0:T(8,128)(2,1)S(1)}, bf16[128,576]{1,0:T(8,128)(2,1)S(1)}, u32[]{:S(2)}, u32[]{:S(2)}) collective-permute-start(bf16[128,576]{1,0:T(8,128)(2,1)S(1)} %copy.276), channel_id=1, source_target_pairs={{0,1},{1,0},{2,3},{3,2},{4,5},{5,4},{6,7},{7,6},{8,9},{9,8},{10,11... | collective-permute-start | bytes 442376 | tf_op jit(solution)/shard_map/ppermute | solution.py:764
  16.9 50.6 %collective-permute-start.2 = (bf16[2,64,2176]{2,1,0:T(8,128)(2,1)S(1)}, bf16[2,64,2176]{2,1,0:T(8,128)(2,1)S(1)}, u32[]{:S(2)}, u32[]{:S(2)}) collective-permute-start(bf16[2,64,2176]{2,1,0:T(8,128)(2,1)S(1)} %fusion.41.refs_0_), channel_id=1, source_target_pairs={{0,6},{1,7},{2,0},{3,1},{4,2},{5,3},{6,4},{7,5},{8,14},{9,15},{10,... | collective-permute-start | bytes 1671176 | tf_op jit(solution)/shard_map/ppermute | solution.py:761
  113.1 725.2 %all-reduce.10.cloned.1.call-start = ((), (), s32[]{:S(2)}) async-start(), calls=%async_computation.3 | async-start | bytes 9437184 | tf_op jit(solution)/shard_map/psum | solution.py:1051
  281.2 90.2 %collective-permute-start.32 = (bf16[2,128,2176]{2,1,0:T(8,128)(2,1)}, bf16[2,128,2176]{2,1,0:T(8,128)(2,1)}, u32[]{:S(2)}, u32[]{:S(2)}) collective-permute-start(bf16[2,128,2176]{2,1,0:T(8,128)(2,1)} %get-tuple-element.132), channel_id=1, source_target_pairs={{0,16},{16,0},{1,17},{17,1},{2,18},{18,2},{3,19},{19,3},{4,20},{20... | collective-permute-start | bytes 3342344 | tf_op jit(solution)/shard_map/ppermute | solution.py:767
  286.1 85.4 %collective-permute-start.33 = (bf16[2,128,2176]{2,1,0:T(8,128)(2,1)}, bf16[2,128,2176]{2,1,0:T(8,128)(2,1)}, u32[]{:S(2)}, u32[]{:S(2)}) collective-permute-start(bf16[2,128,2176]{2,1,0:T(8,128)(2,1)} %get-tuple-element.133), channel_id=1, source_target_pairs={{0,16},{16,0},{1,17},{17,1},{2,18},{18,2},{3,19},{19,3},{4,20},{20... | collective-permute-start | bytes 3342344 | tf_op jit(solution)/shard_map/ppermute | solution.py:767
  296.0 59.3 %collective-permute-start.30 = (bf16[2,128,2048]{2,1,0:T(8,128)(2,1)}, bf16[2,128,2048]{2,1,0:T(8,128)(2,1)}, u32[]{:S(2)}, u32[]{:S(2)}) collective-permute-start(bf16[2,128,2048]{2,1,0:T(8,128)(2,1)} %get-tuple-element.148), channel_id=1, source_target_pairs={{0,16},{16,0},{1,17},{17,1},{2,18},{18,2},{3,19},{19,3},{4,20},{20... | collective-permute-start | bytes 3145736 | tf_op jit(solution)/shard_map/ppermute | solution.py:767
  304.7 66.7 %collective-permute-start.31 = (bf16[2,128,2048]{2,1,0:T(8,128)(2,1)}, bf16[2,128,2048]{2,1,0:T(8,128)(2,1)S(1)}, u32[]{:S(2)}, u32[]{:S(2)}) collective-permute-start(bf16[2,128,2048]{2,1,0:T(8,128)(2,1)} %get-tuple-element.137), channel_id=1, source_target_pairs={{0,16},{16,0},{1,17},{17,1},{2,18},{18,2},{3,19},{19,3},{4,20},{20... | collective-permute-start | bytes 3145736 | tf_op jit(solution)/shard_map/ppermute | solution.py:767
  406.2 52.3 %collective-permute-start.34 = (bf16[2,128,2048]{2,1,0:T(8,128)(2,1)}, bf16[2,128,2048]{2,1,0:T(8,128)(2,1)S(1)}, u32[]{:S(2)}, u32[]{:S(2)}) collective-permute-start(bf16[2,128,2048]{2,1,0:T(8,128)(2,1)} %bitcast.225), channel_id=1, source_target_pairs={{0,16},{16,0},{1,17},{17,1},{2,18},{18,2},{3,19},{19,3},{4,20},{20... | collective-permute-start | bytes 3145736 | tf_op jit(solution)/shard_map/ppermute | solution.py:767
  454.8 66.4 %collective-permute-start.41 = (bf16[2,64,2176]{2,1,0:T(8,128)(2,1)}, bf16[2,64,2176]{2,1,0:T(8,128)(2,1)S(1)}, u32[]{:S(2)}, u32[]{:S(2)}) collective-permute-start(bf16[2,64,2176]{2,1,0:T(8,128)(2,1)} %get-tuple-element.180), channel_id=1, source_target_pairs={{0,1},{1,0},{2,3},{3,2},{4,5},{5,4},{6,7},{7,6},{8,9},{9,8},{10,11... | collective-permute-start | bytes 1671176 | tf_op jit(solution)/shard_map/ppermute | solution.py:764
  503.7 91.3 %collective-permute-start.39 = (bf16[2,128,2048]{2,1,0:T(8,128)(2,1)}, bf16[2,128,2048]{2,1,0:T(8,128)(2,1)}, u32[]{:S(2)}, u32[]{:S(2)}) collective-permute-start(bf16[2,128,2048]{2,1,0:T(8,128)(2,1)} %bitcast.223), channel_id=1, source_target_pairs={{0,16},{16,0},{1,17},{17,1},{2,18},{18,2},{3,19},{19,3},{4,20},{20... | collective-permute-start | bytes 3145736 | tf_op jit(solution)/shard_map/ppermute | solution.py:767
  504.2 78.7 %collective-permute-start.40 = (bf16[2,128,2048]{2,1,0:T(8,128)(2,1)}, bf16[2,128,2048]{2,1,0:T(8,128)(2,1)}, u32[]{:S(2)}, u32[]{:S(2)}) collective-permute-start(bf16[2,128,2048]{2,1,0:T(8,128)(2,1)} %bitcast.224), channel_id=1, source_target_pairs={{0,16},{16,0},{1,17},{17,1},{2,18},{18,2},{3,19},{19,3},{4,20},{20... | collective-permute-start | bytes 3145736 | tf_op jit(solution)/shard_map/ppermute | solution.py:767
  505.8 395.4 %reduce-scatter.2.cloned.1.call-start = ((), (), s32[]{:S(2)}) async-start(), calls=%async_computation.2 | async-start | bytes 4718592 | tf_op jit(solution)/shard_map/reduce_scatter | solution.py:1089
  521.2 82.0 %collective-permute-start.88 = (bf16[704,1024]{1,0:T(8,128)(2,1)}, bf16[704,1024]{1,0:T(8,128)(2,1)}, u32[]{:S(2)}, u32[]{:S(2)}) collective-permute-start(bf16[704,1024]{1,0:T(8,128)(2,1)} %get-tuple-element.220), channel_id=1, source_target_pairs={{0,8},{8,0},{1,9},{9,1},{2,10},{10,2},{3,11},{11,3},{4,12},{12,4},... | collective-permute-start | bytes 4325384 | tf_op jit(solution)/shard_map/ppermute | solution.py:770
  521.4 81.9 %collective-permute-start.87 = (bf16[704,1024]{1,0:T(8,128)(2,1)}, bf16[704,1024]{1,0:T(8,128)(2,1)}, u32[]{:S(2)}, u32[]{:S(2)}) collective-permute-start(bf16[704,1024]{1,0:T(8,128)(2,1)} %get-tuple-element.219), channel_id=1, source_target_pairs={{0,8},{8,0},{1,9},{9,1},{2,10},{10,2},{3,11},{11,3},{4,12},{12,4},... | collective-permute-start | bytes 4325384 | tf_op jit(solution)/shard_map/ppermute | solution.py:770
  526.1 57.1 %collective-permute-start.46 = (bf16[2,64,2048]{2,1,0:T(8,128)(2,1)S(1)}, bf16[2,64,2048]{2,1,0:T(8,128)(2,1)}, u32[]{:S(2)}, u32[]{:S(2)}) collective-permute-start(bf16[2,64,2048]{2,1,0:T(8,128)(2,1)S(1)} %fusion.98.refs_0_), channel_id=1, source_target_pairs={{0,2},{1,3},{2,4},{3,5},{4,6},{5,7},{6,0},{7,1},{8,10},{9,11},{10,... | collective-permute-start | bytes 1572872 | tf_op jit(solution)/shard_map/ppermute | solution.py:761
  595.0 125.5 %collective-permute-start.85 = (bf16[1024,1408]{1,0:T(8,128)(2,1)}, bf16[1024,1408]{1,0:T(8,128)(2,1)}, u32[]{:S(2)}, u32[]{:S(2)}) collective-permute-start(bf16[1024,1408]{1,0:T(8,128)(2,1)} %shard_map.338), channel_id=1, source_target_pairs={{0,8},{8,0},{1,9},{9,1},{2,10},{10,2},{3,11},{11,3},{4,12},{12,4},... | collective-permute-start | bytes 8650760 | tf_op jit(solution)/shard_map/ppermute | solution.py:770
  614.6 50.2 %collective-permute-start.51 = (bf16[2,64,2048]{2,1,0:T(8,128)(2,1)}, bf16[2,64,2048]{2,1,0:T(8,128)(2,1)}, u32[]{:S(2)}, u32[]{:S(2)}) collective-permute-start(bf16[2,64,2048]{2,1,0:T(8,128)(2,1)} %collective-permute-done.47.refs_2_), channel_id=1, source_target_pairs={{0,1},{1,0},{2,3},{3,2},{4,5},{5,4},{6,7},{7,6},{8,9},{9,8},{10,11... | collective-permute-start | bytes 1572872 | tf_op jit(solution)/shard_map/ppermute | solution.py:764
  623.9 121.2 %collective-permute-start.86 = (bf16[1024,1408]{1,0:T(8,128)(2,1)}, bf16[1024,1408]{1,0:T(8,128)(2,1)}, u32[]{:S(2)}, u32[]{:S(2)}) collective-permute-start(bf16[1024,1408]{1,0:T(8,128)(2,1)} %shard_map.340), channel_id=1, source_target_pairs={{0,8},{8,0},{1,9},{9,1},{2,10},{10,2},{3,11},{11,3},{4,12},{12,4},... | collective-permute-start | bytes 8650760 | tf_op jit(solution)/shard_map/ppermute | solution.py:770
  673.9 54.9 %collective-permute-start.82 = (bf16[128,2048]{1,0:T(8,128)(2,1)}, bf16[128,2048]{1,0:T(8,128)(2,1)}, u32[]{:S(2)}, u32[]{:S(2)}) collective-permute-start(bf16[128,2048]{1,0:T(8,128)(2,1)} %constant_dynamic-slice_fusion), channel_id=1, source_target_pairs={{0,8},{8,0},{1,9},{9,1},{2,10},{10,2},{3,11},{11,3},{4,12},{12,4},... | collective-permute-start | bytes 1572872 | tf_op jit(solution)/shard_map/ppermute | solution.py:770
  703.9 51.5 %collective-permute-start.60 = (bf16[2,512,576]{1,2,0:T(8,128)(2,1)}, bf16[2,512,576]{1,2,0:T(8,128)(2,1)}, u32[]{:S(2)}, u32[]{:S(2)}) collective-permute-start(bf16[2,512,576]{1,2,0:T(8,128)(2,1)} %copy.237), channel_id=1, source_target_pairs={{0,8},{8,0},{1,9},{9,1},{2,10},{10,2},{3,11},{11,3},{4,12},{12,4},... | collective-permute-start | bytes 3538952 | tf_op jit(solution)/shard_map/ppermute | solution.py:770
  716.6 92.4 %collective-permute-start.53 = (bf16[2,64,2048]{2,1,0:T(8,128)(2,1)}, bf16[2,64,2048]{2,1,0:T(8,128)(2,1)}, u32[]{:S(2)}, u32[]{:S(2)}) collective-permute-start(bf16[2,64,2048]{2,1,0:T(8,128)(2,1)} %get-tuple-element.188), channel_id=1, source_target_pairs={{0,1},{1,0},{2,3},{3,2},{4,5},{5,4},{6,7},{7,6},{8,9},{9,8},{10,11... | collective-permute-start | bytes 1572872 | tf_op jit(solution)/shard_map/ppermute | solution.py:764
  755.4 56.2 %collective-permute-start.59 = (bf16[2,64,2048]{2,1,0:T(8,128)(2,1)}, bf16[2,64,2048]{2,1,0:T(8,128)(2,1)}, u32[]{:S(2)}, u32[]{:S(2)}) collective-permute-start(bf16[2,64,2048]{2,1,0:T(8,128)(2,1)} %add_convert_fusion.9), channel_id=1, source_target_pairs={{0,2},{1,3},{2,4},{3,5},{4,6},{5,7},{6,0},{7,1},{8,10},{9,11},{10,... | collective-permute-start | bytes 1572872 | tf_op jit(solution)/shard_map/ppermute | solution.py:761
  804.6 46.3 %collective-permute-start.77 = (bf16[1024,384]{1,0:T(8,128)(2,1)}, bf16[1024,384]{1,0:T(8,128)(2,1)}, u32[]{:S(2)}, u32[]{:S(2)}) collective-permute-start(bf16[1024,384]{1,0:T(8,128)(2,1)} %constant_dynamic-slice_fusion.1), channel_id=1, source_target_pairs={{0,8},{8,0},{1,9},{9,1},{2,10},{10,2},{3,11},{11,3},{4,12},{12,4},... | collective-permute-start | bytes 2359304 | tf_op jit(solution)/shard_map/ppermute | solution.py:770
  (163 other events, 3610.2 us)
Sparse Core Ops, SparseCore 0:
  113.2 73.2 all-gather.1
  505.9 122.7 all-reduce.9
  632.3 94.0 reduce-scatter.1
where the time goes:
time: 917 us; the launch traced here: 911 us
  waiting for transfers between devices  354 us (39%)
  Pallas kernels  214 us (23%)
  starting transfers between devices  112 us (12%)
  other arithmetic  89.7 us (10%)
  matrix products  71.2 us (8%)
  local copies, waits for them, and re-layouts  54.9 us (6%)
  between operations  15.5 us (2%)
    ppermute x36, waiting for transfers between devices, across(): return lax.ppermute(value, EXPERT, [(e, e ^ 1) for e in range(n_expert)])  173 us
    ppermute x13, waiting for transfers between devices, other_dp(): return lax.ppermute(value, DP, [(d, n_dp - 1 - d) for d in range(n_dp)])  110 us
    ppermute x27, waiting for transfers between devices, shift(): return lax.ppermute(value, EXPERT, pairs)  70.6 us
    pallas_call x2, Pallas kernels, expert_rows(): pl.pallas_call(functools.partial(expert_kernel, TOP), in_specs=[pl.BlockS...  61.2 us
    ppermute x27, starting transfers between devices, shift(): return lax.ppermute(value, EXPERT, pairs)  47.9 us
    ppermute x36, starting transfers between devices, across(): return lax.ppermute(value, EXPERT, [(e, e ^ 1) for e in range(n_expert)])  47.4 us
    pallas_call x4, Pallas kernels, half_grads(): pl.pallas_call(half_kernel, grid_spec=pltpu.PrefetchScalarGridSpec(num_sc...  30 us
    convert_element_type x18, other arithmetic, add(): return total.astype(BF16)  29.3 us
  transfers between devices with their start and end apart: 92, of which 32 were waited for; matrix products, arithmetic and copies ran while one was open for 22% of the time, Pallas kernels for 20%

commit v1 on v0

--- a/solution.py
+++ b/solution.py
@@ -799,12 +799,13 @@
             total = total + term.astype(F32)
         return total.astype(BF16)
 
-    def scatter_blocks(part, hold=()):
+    def scatter_blocks(part, hold=(), first=()):
         order = [up_count] + [k for k in range(lanes - 1, 0, -1) if k != up_count] + [0]
         crossed = {k: across(part(lanes + k)) for k in order}
         sums = {k: (part(k), crossed[k]) for k in order}
         marks = [crossed[up_count]]
-        moving = add(*sums[up_count])
+        mine, got = sums[up_count]
+        moving = add(after(mine, *first) if first else mine, got)
         for k in range(up_count, 0, -1):
             if k == 1 and hold:
                 moving = after(moving, *hold)
@@ -905,7 +906,12 @@
 
     own_rows = hidden_in.astype(F32)
     inv_own = rms(own_rows)
-    normed_span, routes_cols = join_norm(blocks, norm_attn)
+    normed_span, routes_cols = join_norm(
+        [
+            after(blocks[0], span_cos, span_sin, turns, w_inner, w_shared, w_shared_down),
+            *blocks[1:],
+        ], norm_attn
+    )
     grad_all = lax.all_gather(after(out_grad, normed_span), EXPERT, axis=1, tiled=True)
     kv_joint = product(normed_span, kv_full)
     latent_raw = kv_joint[..., :LATENT]
@@ -1032,18 +1038,19 @@
             columns = columns + jnp.where(lane_ids == target + expert_count, rows - top, 0.0)
         return columns.astype(BF16)
 
-    dnorm_blocks = [
-        spread_blocks(
-            sh_dnorm,
-            side,
-            near_tables[side],
-            near_dx[side],
-            far_tables[side],
-            dx_back[side],
-            dg_columns(side),
+    dnorm_blocks = []
+    for side in range(2):
+        dnorm_blocks.append(
+            spread_blocks(
+                sh_dnorm,
+                side,
+                near_tables[side],
+                near_dx[side],
+                far_tables[side],
+                dx_back[side],
+                dg_columns(side),
+            )
         )
-        for side in range(2)
-    ]
     dnorm_sum, marks = scatter_blocks(lambda j: dnorm_blocks[j // lanes][j % lanes])
 
     grad_sh_in = weight_grad(sh_dboth, ffn_span).astype(BF16)
@@ -1133,7 +1140,9 @@
     grad_latent_span = jnp.concatenate(
         [scatter_ctx(grad_latent), early.reshape(seqs, span, ROPE)], axis=-1
     )
-    dnorm_own, marks = scatter_blocks(project_sides(grad_queries, w_query, True))
+    dnorm_own, marks = scatter_blocks(
+        project_sides(grad_queries, w_query, True), first=(grad_latent_span,)
+    )
     grad_latent_own, lat_marks = scatter_blocks(lambda j: block_of_span(grad_latent_span, j))
     early = grad_latent_own[..., LATENT + ROPE :].reshape(-1)[:early_size]
 
@@ -1147,7 +1156,7 @@
         exp_grads = []
         for i in range(2):
             exp_grads.append(
-                half_grads(far[0], near[0], far[3 + i], near[3 + i], after(rank, marks[0]), got[i])
+                half_grads(far[0], near[0], far[3 + i], near[3 + i], rank, got[i])
             )
     gain_part = jnp.sum(grad_query_part * w_query.astype(F32), axis=-1) / norm_attn
     gain_latent_part = jnp.sum(grad_up_part * w_up.astype(F32), axis=-1) / norm_latent
@@ -1167,14 +1176,15 @@
     kv_grads = gather_blocks(jnp.concatenate([grad_kv, late], axis=-1))
     grad_kv_span = join(kv_grads)
     shared_sums = lax.optimization_barrier(
-        (grad_sh_in, grad_sh_down, kv_grads[lanes + up_count])
+        (grad_sh_in, grad_sh_down, kv_grads[lanes])
     )[:2]
+    shared_grads = [
+        shared_sums[0][:shared_width].astype(F32).T,
+        shared_sums[0][shared_room : shared_room + shared_width].astype(F32).T,
+        shared_sums[1][:shared_width].astype(F32),
+    ]
     if n_ctx == 2:
         exp_grads.append(merge_down(*down_mine, *got[2:]))
-    dnorm_kv = back_product(grad_kv, kv_full)
-    in_grad = (
-        grad_resid + norm_back(dnorm_own + dnorm_kv, own_rows, inv_own, norm_attn)
-    ).astype(BF16)
     normed_cols = lax.dynamic_slice_in_dim(normed_span, expert_rank * kv_rows, kv_rows, 2)
     late = (
         grad_kv_span[..., LATENT + ROPE :]
@@ -1188,12 +1198,19 @@
     )
     rows = width // n_expert
     small = padded(jnp.concatenate([late, early])[None], kv_rows * ROPE).reshape(kv_rows, ROPE)
-    kv_small = sum_copies(
-        jnp.concatenate(
-            [weight_grad(normed_cols, grad_kv_span[..., : LATENT + ROPE]), small], axis=-1
-        ),
-        small=True,
-    )
+    kv_part = jnp.concatenate(
+        [weight_grad(normed_cols, grad_kv_span[..., : LATENT + ROPE]), small], axis=-1
+    ).astype(BF16)
+    if n_ctx == 2:
+        kv_pair = add(kv_part, other_ctx(kv_part))
+        kv_small = kv_pair.astype(F32) + other_dp(kv_pair).astype(F32)
+    else:
+        kv_pair = kv_part
+        kv_small = lax.psum(kv_part, (DP, CTX)).astype(F32)
+    dnorm_kv = back_product(after(grad_kv, kv_pair), kv_full)
+    in_grad = (
+        grad_resid + norm_back(dnorm_own + dnorm_kv, own_rows, inv_own, norm_attn)
+    ).astype(BF16)
     grad_kv_w = kv_small[:, : LATENT + ROPE]
     small = kv_small[:, LATENT + ROPE :].reshape(-1)
     late, early = small[:late_size], small[late_size : late_size + early_size]
@@ -1211,9 +1228,7 @@
         grad_out_w,
         early[:rows],
         early[rows:].reshape(rows, expert_count),
-        shared_sums[0][:shared_width].astype(F32).T,
-        shared_sums[0][shared_room : shared_room + shared_width].astype(F32).T,
-        shared_sums[1][:shared_width].astype(F32),
+        *shared_grads,
         exp_grads[0][None],
         exp_grads[1][None],
         exp_grads[2][None],

time: 917 us -> 901 us (0.983)
    ppermute x36, waiting for transfers between devices: 173 us -> 146 us  [across(): return lax.ppermute(value, EXPERT, [(e, e ^ 1) for e in range(n_expert)])]
    ppermute x13, waiting for transfers between devices: 110 us -> 121 us  [other_dp(): return lax.ppermute(value, DP, [(d, n_dp - 1 - d) for d in range(n_dp)])]
  transfers between devices with their start and end apart: 92 -> 92, of which waited for: 32 -> 33; matrix products, arithmetic and copies ran while one was open for 22% -> 22% of each run, Pallas kernels for 20% -> 21%
where the time goes in v1:
time: 901 us; the launch traced here: 893 us
  waiting for transfers between devices  345 us (38%)
  Pallas kernels  214 us (24%)
  starting transfers between devices  107 us (12%)
  other arithmetic  89 us (10%)
  matrix products  71.9 us (8%)
  local copies, waits for them, and re-layouts  50.2 us (6%)
  between operations  15.6 us (2%)
    ppermute x36, waiting for transfers between devices, across(): return lax.ppermute(value, EXPERT, [(e, e ^ 1) for e in range(n_expert)])  146 us
    ppermute x13, waiting for transfers between devices, other_dp(): return lax.ppermute(value, DP, [(d, n_dp - 1 - d) for d in range(n_dp)])  121 us
    ppermute x27, waiting for transfers between devices, shift(): return lax.ppermute(value, EXPERT, pairs)  77.3 us
    pallas_call x2, Pallas kernels, expert_rows(): pl.pallas_call(functools.partial(expert_kernel, TOP), in_specs=[pl.BlockS...  61.4 us
    ppermute x27, starting transfers between devices, shift(): return lax.ppermute(value, EXPERT, pairs)  51.5 us
    ppermute x36, starting transfers between devices, across(): return lax.ppermute(value, EXPERT, [(e, e ^ 1) for e in range(n_expert)])  39.6 us
    pallas_call x4, Pallas kernels, half_grads(): pl.pallas_call(half_kernel, grid_spec=pltpu.PrefetchScalarGridSpec(num_sc...  30.1 us
    convert_element_type x18, other arithmetic, add(): return total.astype(BF16)  27.2 us
  transfers between devices with their start and end apart: 92, of which 33 were waited for; matrix products, arithmetic and copies ran while one was open for 22% of the time, Pallas kernels for 21%

profile of v1, /device:TPU:0, one launch (start us, length us, event | category | flops | bytes accessed | tf_op | source)
XLA Modules:
  0.0 892.7 jit_solution(9169999861679796678)
XLA Ops:
  32.8 14.6 %collective-permute-done.refs_1_ = bf16[2,64,2176]{2,1,0:T(8,128)(2,1)} collective-permute-done((bf16[2,64,2176]{2,1,0:T(8,128)(2,1)S(1)}, bf16[2,64,2176]{2,1,0:T(8,128)(2,1)}, u32[]{:S(2)}, u32[]{:S(2)}) %collective-permute-start) | collective-permute-done | bytes 557088 | tf_op jit(solution)/shard_map/ppermute | solution.py:761
  51.2 15.1 %collective-permute-done.8 = bf16[128,576]{1,0:T(8,128)(2,1)S(1)} collective-permute-done((bf16[128,576]{1,0:T(8,128)(2,1)}, bf16[128,576]{1,0:T(8,128)(2,1)S(1)}, u32[]{:S(2)}, u32[]{:S(2)}) %collective-permute-start.8) | collective-permute-done | bytes 147488 | tf_op jit(solution)/shard_map/ppermute | solution.py:761
  85.4 23.9 %collective-permute-done.6.refs_7_ = bf16[2,64,2176]{2,1,0:T(8,128)(2,1)} collective-permute-done((bf16[2,64,2176]{2,1,0:T(8,128)(2,1)}, bf16[2,64,2176]{2,1,0:T(8,128)(2,1)}, u32[]{:S(2)}, u32[]{:S(2)}) %collective-permute-start.6) | collective-permute-done | bytes 557088 | tf_op jit(solution)/shard_map/ppermute | solution.py:764
  109.3 9.0 %collective-permute-done.5.refs_6_ = bf16[2,64,2176]{2,1,0:T(8,128)(2,1)} collective-permute-done((bf16[2,64,2176]{2,1,0:T(8,128)(2,1)}, bf16[2,64,2176]{2,1,0:T(8,128)(2,1)}, u32[]{:S(2)}, u32[]{:S(2)}) %collective-permute-start.5) | collective-permute-done | bytes 557088 | tf_op jit(solution)/shard_map/ppermute | solution.py:764
  159.2 12.7 %shard_map.317 = (bf16[2,512,256]{2,1,0:T(8,128)(2,1)}, f32[2,2,512]{2,1,0:T(2,128)}) custom-call(bf16[2,512,384]{2,1,0:T(8,128)(2,1)} %pad_maximum_fusion.7.q_ref, bf16[2,1024,512]{2,1,0:T(8,128)(2,1)} %convolution_convert_fusion.3.k_ref.v_ref, bf16[2,1024,512]{2,1,0:T(8,128)(2,1)} %convolution_convert_fusion.3.k_ref.v_ref, ...), custom_call_target="tpu_custom_call" | custom-call | flops 1342177280 | bytes 2883584 | tf_op jit(solution)/shard_map/pallas_call | solution.py:184
  181.8 8.5 collective-permute-done.18
  196.0 16.7 %collective-permute-done.21 = bf16[2,64,2048]{2,1,0:T(8,128)(2,1)S(1)} collective-permute-done((bf16[2,64,2048]{2,1,0:T(8,128)(2,1)}, bf16[2,64,2048]{2,1,0:T(8,128)(2,1)S(1)}, u32[]{:S(2)}, u32[]{:S(2)}) %collective-permute-start.21) | collective-permute-done | bytes 524320 | tf_op jit(solution)/shard_map/ppermute | solution.py:764
  234.1 10.7 %collective-permute-done.20 = bf16[2,64,2048]{2,1,0:T(8,128)(2,1)S(1)} collective-permute-done((bf16[2,64,2048]{2,1,0:T(8,128)(2,1)S(1)}, bf16[2,64,2048]{2,1,0:T(8,128)(2,1)S(1)}, u32[]{:S(2)}, u32[]{:S(2)}) %collective-permute-start.20) | collective-permute-done | bytes 524320 | tf_op jit(solution)/shard_map/ppermute | solution.py:761
  250.7 12.7 %collective-permute-done.24.refs_1_ = bf16[2,64,2048]{2,1,0:T(8,128)(2,1)S(1)} collective-permute-done((bf16[2,64,2048]{2,1,0:T(8,128)(2,1)S(1)}, bf16[2,64,2048]{2,1,0:T(8,128)(2,1)S(1)}, u32[]{:S(2)}, u32[]{:S(2)}) %collective-permute-start.24) | collective-permute-done | bytes 524320 | tf_op jit(solution)/shard_map/ppermute | solution.py:761
  273.2 10.4 %collective-permute-done.26.refs_2_ = bf16[2,64,2048]{2,1,0:T(8,128)(2,1)S(1)} collective-permute-done((bf16[2,64,2048]{2,1,0:T(8,128)(2,1)S(1)}, bf16[2,64,2048]{2,1,0:T(8,128)(2,1)S(1)}, u32[]{:S(2)}, u32[]{:S(2)}) %collective-permute-start.26) | collective-permute-done | bytes 524320 | tf_op jit(solution)/shard_map/ppermute | solution.py:761
  290.1 11.1 %collective-permute-done.29.refs_3_.refs_7_ = bf16[2,64,2048]{2,1,0:T(8,128)(2,1)} collective-permute-done((bf16[2,64,2048]{2,1,0:T(8,128)(2,1)S(1)}, bf16[2,64,2048]{2,1,0:T(8,128)(2,1)}, u32[]{:S(2)}, u32[]{:S(2)}) %collective-permute-start.29) | collective-permute-done | bytes 524320 | tf_op jit(solution)/shard_map/ppermute | solution.py:764
  334.1 24.1 %collective-permute-done.30 = bf16[2,128,2048]{2,1,0:T(8,128)(2,1)} collective-permute-done((bf16[2,128,2048]{2,1,0:T(8,128)(2,1)}, bf16[2,128,2048]{2,1,0:T(8,128)(2,1)}, u32[]{:S(2)}, u32[]{:S(2)}) %collective-permute-start.30) | collective-permute-done | bytes 1048608 | tf_op jit(solution)/shard_map/ppermute | solution.py:767
  358.2 17.4 %collective-permute-done.31 = bf16[2,128,2048]{2,1,0:T(8,128)(2,1)S(1)} collective-permute-done((bf16[2,128,2048]{2,1,0:T(8,128)(2,1)}, bf16[2,128,2048]{2,1,0:T(8,128)(2,1)S(1)}, u32[]{:S(2)}, u32[]{:S(2)}) %collective-permute-start.31) | collective-permute-done | bytes 1048608 | tf_op jit(solution)/shard_map/ppermute | solution.py:767
  376.6 30.8 %shard_map.326 = (bf16[512,2048]{1,0:T(8,128)(2,1)}, bf16[512,2048]{1,0:T(8,128)(2,1)}, bf16[512,1408]{1,0:T(8,128)(2,1)}, bf16[512,1408]{1,0:T(8,128)(2,1)}, bf...) custom-call(s32[1]{0:T(128)} %bitcast.39.mine_ref, ...), custom_call_target="tpu_custom_call" | custom-call | flops 17716740096 | bytes 38404096 | tf_op jit(solution)/shard_map/pallas_call | solution.py:598
  412.0 30.6 %shard_map.327 = (bf16[512,2048]{1,0:T(8,128)(2,1)}, bf16[512,2048]{1,0:T(8,128)(2,1)}, bf16[512,1408]{1,0:T(8,128)(2,1)}, bf16[512,1408]{1,0:T(8,128)(2,1)}, bf...) custom-call(s32[1]{0:T(128)} %bitcast.39.mine_ref, ...), custom_call_target="tpu_custom_call" | custom-call | flops 17716740096 | bytes 38404096 | tf_op jit(solution)/shard_map/pallas_call | solution.py:598
  475.9 20.8 %collective-permute-done.44 = bf16[2,64,2176]{2,1,0:T(8,128)(2,1)} collective-permute-done((bf16[2,64,2176]{2,1,0:T(8,128)(2,1)}, bf16[2,64,2176]{2,1,0:T(8,128)(2,1)}, u32[]{:S(2)}, u32[]{:S(2)}) %collective-permute-start.44) | collective-permute-done | bytes 557088 | tf_op jit(solution)/shard_map/ppermute | solution.py:764
  530.7 26.1 %collective-permute-done.39.refs_4_ = bf16[2,128,2048]{2,1,0:T(8,128)(2,1)S(1)} collective-permute-done((bf16[2,128,2048]{2,1,0:T(8,128)(2,1)}, bf16[2,128,2048]{2,1,0:T(8,128)(2,1)S(1)}, u32[]{:S(2)}, u32[]{:S(2)}) %collective-permute-start.39) | collective-permute-done | bytes 1048608 | tf_op jit(solution)/shard_map/ppermute | solution.py:767
  559.8 30.4 %collective-permute-done.40.refs_4_ = bf16[2,128,2048]{2,1,0:T(8,128)(2,1)} collective-permute-done((bf16[2,128,2048]{2,1,0:T(8,128)(2,1)}, bf16[2,128,2048]{2,1,0:T(8,128)(2,1)}, u32[]{:S(2)}, u32[]{:S(2)}) %collective-permute-start.40) | collective-permute-done | bytes 1048608 | tf_op jit(solution)/shard_map/ppermute | solution.py:767
  633.9 8.2 shard_map.339
  642.1 8.0 shard_map.341
  663.2 16.0 %shard_map.334 = (bf16[2,512,384]{2,1,0:T(8,128)(2,1)}, bf16[2,1024,512]{2,1,0:T(8,128)(2,1)}, bf16[2,1024,64]{2,1,0:T(8,128)(2,1)}) custom-call(bf16[2,512,384]{2,1,0:T(8,128)(2,1)} %pad_maximum_fusion.7.q_ref, bf16[2,1024,512]{2,1,0:T(8,128)(2,1)} %convolution_convert_fusion.3.k_ref.v_ref, bf16[2,1024,512]{2,1,0:T(8,128)(2,1)} %convolution_convert_fusion.3.k_ref.v_ref, ...), custom_call_target="tpu_custom_call" | custom-call | flops 2684354560 | bytes 4980736 | tf_op jit(solution)/shard_map/pallas_call | solution.py:218
  700.1 24.2 %collective-permute-done.56 = bf16[2,64,2048]{2,1,0:T(8,128)(2,1)} collective-permute-done((bf16[2,64,2048]{2,1,0:T(8,128)(2,1)}, bf16[2,64,2048]{2,1,0:T(8,128)(2,1)}, u32[]{:S(2)}, u32[]{:S(2)}) %collective-permute-start.56) | collective-permute-done | bytes 524320 | tf_op jit(solution)/shard_map/ppermute | solution.py:764
  728.9 7.6 collective-permute-done.59
  847.9 18.1 %collective-permute-done.76 = bf16[256,640]{0,1:T(8,128)(2,1)} collective-permute-done((bf16[256,640]{0,1:T(8,128)(2,1)}, bf16[256,640]{0,1:T(8,128)(2,1)}, u32[]{:S(2)}, u32[]{:S(2)}) %collective-permute-start.76) | collective-permute-done | bytes 327712 | tf_op jit(solution)/shard_map/ppermute | solution.py:767
  (597 shorter events, 469.5 us)
Async XLA Ops:
  7.2 208.3 %all-gather.2.cloned.1.call-start = ((), (), s32[]{:S(2)}) async-start(), calls=%async_computation.1 | async-start | bytes 4718592 | tf_op jit(solution)/shard_map/all_gather | solution.py:915
  17.5 51.8 %collective-permute-start.2 = (bf16[2,64,2176]{2,1,0:T(8,128)(2,1)S(1)}, bf16[2,64,2176]{2,1,0:T(8,128)(2,1)}, u32[]{:S(2)}, u32[]{:S(2)}) collective-permute-start(bf16[2,64,2176]{2,1,0:T(8,128)(2,1)S(1)} %fusion.41.refs_0_), channel_id=1, source_target_pairs={{0,6},{1,7},{2,0},{3,1},{4,2},{5,3},{6,4},{7,5},{8,14},{9,15},{10,... | collective-permute-start | bytes 1671176 | tf_op jit(solution)/shard_map/ppermute | solution.py:761
  70.8 47.5 %collective-permute-start.5 = (bf16[2,64,2176]{2,1,0:T(8,128)(2,1)}, bf16[2,64,2176]{2,1,0:T(8,128)(2,1)}, u32[]{:S(2)}, u32[]{:S(2)}) collective-permute-start(bf16[2,64,2176]{2,1,0:T(8,128)(2,1)} %collective-permute-done.1.refs_2_), channel_id=1, source_target_pairs={{0,1},{1,0},{2,3},{3,2},{4,5},{5,4},{6,7},{7,6},{8,9},{9,8},{10,11... | collective-permute-start | bytes 1671176 | tf_op jit(solution)/shard_map/ppermute | solution.py:764
  78.9 47.1 %collective-permute-start.14 = (bf16[1,1024,576]{1,2,0:T(8,128)(2,1)}, bf16[1,1024,576]{1,2,0:T(8,128)(2,1)}, u32[]{:S(2)}, u32[]{:S(2)}) collective-permute-start(bf16[1,1024,576]{1,2,0:T(8,128)(2,1)} %copy.218), channel_id=1, source_target_pairs={{0,8},{8,0},{1,9},{9,1},{2,10},{10,2},{3,11},{11,3},{4,12},{12,4},... | collective-permute-start | bytes 3538952 | tf_op jit(solution)/shard_map/ppermute | solution.py:770
  123.1 670.6 %all-reduce.10.cloned.1.call-start = ((), (), s32[]{:S(2)}) async-start(), calls=%async_computation.3 | async-start | bytes 9437184 | tf_op jit(solution)/shard_map/psum | solution.py:1058
  284.0 91.6 %collective-permute-start.32 = (bf16[2,128,2176]{2,1,0:T(8,128)(2,1)}, bf16[2,128,2176]{2,1,0:T(8,128)(2,1)}, u32[]{:S(2)}, u32[]{:S(2)}) collective-permute-start(bf16[2,128,2176]{2,1,0:T(8,128)(2,1)} %get-tuple-element.136), channel_id=1, source_target_pairs={{0,16},{16,0},{1,17},{17,1},{2,18},{18,2},{3,19},{19,3},{4,20},{20... | collective-permute-start | bytes 3342344 | tf_op jit(solution)/shard_map/ppermute | solution.py:767
  289.6 86.0 %collective-permute-start.33 = (bf16[2,128,2176]{2,1,0:T(8,128)(2,1)}, bf16[2,128,2176]{2,1,0:T(8,128)(2,1)}, u32[]{:S(2)}, u32[]{:S(2)}) collective-permute-start(bf16[2,128,2176]{2,1,0:T(8,128)(2,1)} %get-tuple-element.137), channel_id=1, source_target_pairs={{0,16},{16,0},{1,17},{17,1},{2,18},{18,2},{3,19},{19,3},{4,20},{20... | collective-permute-start | bytes 3342344 | tf_op jit(solution)/shard_map/ppermute | solution.py:767
  301.2 57.0 %collective-permute-start.30 = (bf16[2,128,2048]{2,1,0:T(8,128)(2,1)}, bf16[2,128,2048]{2,1,0:T(8,128)(2,1)}, u32[]{:S(2)}, u32[]{:S(2)}) collective-permute-start(bf16[2,128,2048]{2,1,0:T(8,128)(2,1)} %get-tuple-element.151), channel_id=1, source_target_pairs={{0,16},{16,0},{1,17},{17,1},{2,18},{18,2},{3,19},{19,3},{4,20},{20... | collective-permute-start | bytes 3145736 | tf_op jit(solution)/shard_map/ppermute | solution.py:767
  309.8 65.8 %collective-permute-start.31 = (bf16[2,128,2048]{2,1,0:T(8,128)(2,1)}, bf16[2,128,2048]{2,1,0:T(8,128)(2,1)S(1)}, u32[]{:S(2)}, u32[]{:S(2)}) collective-permute-start(bf16[2,128,2048]{2,1,0:T(8,128)(2,1)} %get-tuple-element.141), channel_id=1, source_target_pairs={{0,16},{16,0},{1,17},{17,1},{2,18},{18,2},{3,19},{19,3},{4,20},{20... | collective-permute-start | bytes 3145736 | tf_op jit(solution)/shard_map/ppermute | solution.py:767
  410.6 47.3 %collective-permute-start.34 = (bf16[2,128,2048]{2,1,0:T(8,128)(2,1)}, bf16[2,128,2048]{2,1,0:T(8,128)(2,1)S(1)}, u32[]{:S(2)}, u32[]{:S(2)}) collective-permute-start(bf16[2,128,2048]{2,1,0:T(8,128)(2,1)} %bitcast.223), channel_id=1, source_target_pairs={{0,16},{16,0},{1,17},{17,1},{2,18},{18,2},{3,19},{19,3},{4,20},{20... | collective-permute-start | bytes 3145736 | tf_op jit(solution)/shard_map/ppermute | solution.py:767
  463.2 64.0 %collective-permute-start.41 = (bf16[2,64,2176]{2,1,0:T(8,128)(2,1)}, bf16[2,64,2176]{2,1,0:T(8,128)(2,1)S(1)}, u32[]{:S(2)}, u32[]{:S(2)}) collective-permute-start(bf16[2,64,2176]{2,1,0:T(8,128)(2,1)} %get-tuple-element.183), channel_id=1, source_target_pairs={{0,1},{1,0},{2,3},{3,2},{4,5},{5,4},{6,7},{7,6},{8,9},{9,8},{10,11... | collective-permute-start | bytes 1671176 | tf_op jit(solution)/shard_map/ppermute | solution.py:764
  511.2 45.6 %collective-permute-start.39 = (bf16[2,128,2048]{2,1,0:T(8,128)(2,1)}, bf16[2,128,2048]{2,1,0:T(8,128)(2,1)S(1)}, u32[]{:S(2)}, u32[]{:S(2)}) collective-permute-start(bf16[2,128,2048]{2,1,0:T(8,128)(2,1)} %bitcast.222), channel_id=1, source_target_pairs={{0,16},{16,0},{1,17},{17,1},{2,18},{18,2},{3,19},{19,3},{4,20},{20... | collective-permute-start | bytes 3145736 | tf_op jit(solution)/shard_map/ppermute | solution.py:767
  511.8 78.4 %collective-permute-start.40 = (bf16[2,128,2048]{2,1,0:T(8,128)(2,1)}, bf16[2,128,2048]{2,1,0:T(8,128)(2,1)}, u32[]{:S(2)}, u32[]{:S(2)}) collective-permute-start(bf16[2,128,2048]{2,1,0:T(8,128)(2,1)} %bitcast.221), channel_id=1, source_target_pairs={{0,16},{16,0},{1,17},{17,1},{2,18},{18,2},{3,19},{19,3},{4,20},{20... | collective-permute-start | bytes 3145736 | tf_op jit(solution)/shard_map/ppermute | solution.py:767
  513.2 369.7 %reduce-scatter.2.cloned.1.call-start = ((), (), s32[]{:S(2)}) async-start(), calls=%async_computation.2 | async-start | bytes 4718592 | tf_op jit(solution)/shard_map/reduce_scatter | solution.py:1096
  527.2 80.4 %collective-permute-start.88 = (bf16[704,1024]{1,0:T(8,128)(2,1)}, bf16[704,1024]{1,0:T(8,128)(2,1)}, u32[]{:S(2)}, u32[]{:S(2)}) collective-permute-start(bf16[704,1024]{1,0:T(8,128)(2,1)} %get-tuple-element.224), channel_id=1, source_target_pairs={{0,8},{8,0},{1,9},{9,1},{2,10},{10,2},{3,11},{11,3},{4,12},{12,4},... | collective-permute-start | bytes 4325384 | tf_op jit(solution)/shard_map/ppermute | solution.py:770
  527.3 80.3 %collective-permute-start.87 = (bf16[704,1024]{1,0:T(8,128)(2,1)}, bf16[704,1024]{1,0:T(8,128)(2,1)}, u32[]{:S(2)}, u32[]{:S(2)}) collective-permute-start(bf16[704,1024]{1,0:T(8,128)(2,1)} %get-tuple-element.223), channel_id=1, source_target_pairs={{0,8},{8,0},{1,9},{9,1},{2,10},{10,2},{3,11},{11,3},{4,12},{12,4},... | collective-permute-start | bytes 4325384 | tf_op jit(solution)/shard_map/ppermute | solution.py:770
  528.2 103.8 %collective-permute-start.85 = (bf16[1024,1408]{1,0:T(8,128)(2,1)}, bf16[1024,1408]{1,0:T(8,128)(2,1)}, u32[]{:S(2)}, u32[]{:S(2)}) collective-permute-start(bf16[1024,1408]{1,0:T(8,128)(2,1)} %shard_map.338), channel_id=1, source_target_pairs={{0,8},{8,0},{1,9},{9,1},{2,10},{10,2},{3,11},{11,3},{4,12},{12,4},... | collective-permute-start | bytes 8650760 | tf_op jit(solution)/shard_map/ppermute | solution.py:770
  557.7 84.4 %collective-permute-start.86 = (bf16[1024,1408]{1,0:T(8,128)(2,1)}, bf16[1024,1408]{1,0:T(8,128)(2,1)}, u32[]{:S(2)}, u32[]{:S(2)}) collective-permute-start(bf16[1024,1408]{1,0:T(8,128)(2,1)} %shard_map.340), channel_id=1, source_target_pairs={{0,8},{8,0},{1,9},{9,1},{2,10},{10,2},{3,11},{11,3},{4,12},{12,4},... | collective-permute-start | bytes 8650760 | tf_op jit(solution)/shard_map/ppermute | solution.py:770
  684.9 53.6 %collective-permute-start.55 = (bf16[2,512,576]{1,2,0:T(8,128)(2,1)}, bf16[2,512,576]{1,2,0:T(8,128)(2,1)}, u32[]{:S(2)}, u32[]{:S(2)}) collective-permute-start(bf16[2,512,576]{1,2,0:T(8,128)(2,1)} %copy.237), channel_id=1, source_target_pairs={{0,8},{8,0},{1,9},{9,1},{2,10},{10,2},{3,11},{11,3},{4,12},{12,4},... | collective-permute-start | bytes 3538952 | tf_op jit(solution)/shard_map/ppermute | solution.py:770
  689.4 63.7 %collective-permute-start.54 = (bf16[2,64,2048]{2,1,0:T(8,128)(2,1)}, bf16[2,64,2048]{2,1,0:T(8,128)(2,1)}, u32[]{:S(2)}, u32[]{:S(2)}) collective-permute-start(bf16[2,64,2048]{2,1,0:T(8,128)(2,1)} %get-tuple-element.193), channel_id=1, source_target_pairs={{0,1},{1,0},{2,3},{3,2},{4,5},{5,4},{6,7},{7,6},{8,9},{9,8},{10,11... | collective-permute-start | bytes 1572872 | tf_op jit(solution)/shard_map/ppermute | solution.py:764
  692.0 44.6 %collective-permute-start.59 = (bf16[2,64,2048]{2,1,0:T(8,128)(2,1)}, bf16[2,64,2048]{2,1,0:T(8,128)(2,1)}, u32[]{:S(2)}, u32[]{:S(2)}) collective-permute-start(bf16[2,64,2048]{2,1,0:T(8,128)(2,1)} %get-tuple-element.202), channel_id=1, source_target_pairs={{0,1},{1,0},{2,3},{3,2},{4,5},{5,4},{6,7},{7,6},{8,9},{9,8},{10,11... | collective-permute-start | bytes 1572872 | tf_op jit(solution)/shard_map/ppermute | solution.py:764
  700.0 45.8 %collective-permute-start.83 = (bf16[128,2048]{1,0:T(8,128)(2,1)}, bf16[128,2048]{1,0:T(8,128)(2,1)}, u32[]{:S(2)}, u32[]{:S(2)}) collective-permute-start(bf16[128,2048]{1,0:T(8,128)(2,1)} %add_convert_fusion.7), channel_id=1, source_target_pairs={{0,16},{16,0},{1,17},{17,1},{2,18},{18,2},{3,19},{19,3},{4,20},{20... | collective-permute-start | bytes 1572872 | tf_op jit(solution)/shard_map/ppermute | solution.py:767
  771.4 54.8 %collective-permute-start.80 = (bf16[512,512]{0,1:T(8,128)(2,1)}, bf16[512,512]{0,1:T(8,128)(2,1)}, u32[]{:S(2)}, u32[]{:S(2)}) collective-permute-start(bf16[512,512]{0,1:T(8,128)(2,1)} %get-tuple-element.355), channel_id=1, source_target_pairs={{0,8},{8,0},{1,9},{9,1},{2,10},{10,2},{3,11},{11,3},{4,12},{12,4},... | collective-permute-start | bytes 1572872 | tf_op jit(solution)/shard_map/ppermute | solution.py:770
  779.6 48.2 %collective-permute-start.77 = (bf16[1024,384]{1,0:T(8,128)(2,1)}, bf16[1024,384]{1,0:T(8,128)(2,1)}, u32[]{:S(2)}, u32[]{:S(2)}) collective-permute-start(bf16[1024,384]{1,0:T(8,128)(2,1)} %constant_dynamic-slice_fusion.1), channel_id=1, source_target_pairs={{0,8},{8,0},{1,9},{9,1},{2,10},{10,2},{3,11},{11,3},{4,12},{12,4},... | collective-permute-start | bytes 2359304 | tf_op jit(solution)/shard_map/ppermute | solution.py:770
  (166 other events, 3574.0 us)
Sparse Core Ops, SparseCore 0:
  123.2 73.3 all-gather.1
  513.4 123.2 all-reduce.9
  640.3 103.8 reduce-scatter.1
